TPU v7x, 32 devices: a whole 2x2x4 slice. The times are simulated.
32 devices in a mesh: bin: 4 (over z), row: 2 (over y), col: 4 (over x, core).
Axes of the slice: x: 2, y: 2, z: 4, core: 2. Of those that a mesh axis runs over, the one named last changes fastest.
Arguments:
- responses: bfloat16 [2, 4, 4096, 4096], P(None, 'bin', 'row', 'col'), may hold values from -6 to 6
- focusing: bfloat16 [2, 4, 16, 256, 256], P(None, 'bin', 'row'), may hold values from -0.25 to 0.25
- panel: bfloat16 [2, 4096, 256], P(None, 'col'), may hold values from -0.03125 to 0.03125
Outputs:
- projected: float32 [2, 256, 4096], P(None, 'col', 'row')
All inputs are finite; a program needn't handle non-finite values.
Results may differ from a plain program's by a relative error of at most 0.0041.
Values may be sent and summed in bfloat16 or wider, within the bound.
No kernel may reach another device: no remote copies, remote signals or barrier semaphores. Data moves between devices by JAX's collectives and lax.ppermute only.
A program may use at most 128 MiB of HBM per device.

v0:
```python
import functools

import jax
import jax.numpy as jnp
from jax import lax
from jax.experimental import pallas as pl
from jax.experimental.pallas import tpu as pltpu
from jax.sharding import PartitionSpec as P


SPLIT = (1, 1, 1, 1)
HALVED = (0, 1, 2, 3)
TILE = 512
BF16, F32 = jnp.bfloat16, jnp.float32
FIRST = F32


def mm(a, b, ca, cb):
    return lax.dot_general(a, b, (((ca,), (cb,)), ((), ())), preferred_element_type=F32)


VMEM = pl.BlockSpec(memory_space=pltpu.VMEM)
HBM = pl.BlockSpec(memory_space=pltpu.HBM)
SMALL = pltpu.CompilerParams(vmem_limit_bytes=8 * 2**20)
PARAMS = pltpu.CompilerParams(vmem_limit_bytes=20 * 2**20)


def in_vmem(value):
    return pltpu.with_memory_space_constraint(value, pltpu.VMEM)


def in_hbm(value):
    return pltpu.with_memory_space_constraint(value, pltpu.HBM)


def left_kernel(g_ref, first_ref, r_hbm, o_ref, second_ref, sem):
    blocks, size = g_ref.shape[1], g_ref.shape[2]
    head = first_ref.shape[1]
    copy = pltpu.make_async_copy(r_hbm.at[:, pl.ds(head, second_ref.shape[1]), :], second_ref, sem)
    copy.start()
    for j in range(blocks):
        if j * size == head:
            copy.wait()
        g_re, g_im = g_ref[0, j], g_ref[1, j]
        rows = pl.ds(j * size, size)
        src = first_ref if j * size < head else second_ref
        at = pl.ds(j * size if j * size < head else j * size - head, size)
        g = jnp.concatenate([jnp.concatenate([g_re, -g_im], 1), jnp.concatenate([g_im, g_re], 1)], 0)
        r = jnp.concatenate([src[0, at, :], src[1, at, :]], 0)
        y = mm(g, r, 1, 0)
        o_ref[0, :, rows] = y[:size].T.astype(BF16)
        o_ref[1, :, rows] = y[size:].T.astype(BF16)


def left_focus(focusing, first, responses):
    size = focusing.shape[2]
    _, rows, cols = responses.shape
    return pl.pallas_call(
        left_kernel,
        in_specs=[VMEM, VMEM, HBM],
        out_specs=VMEM,
        out_shape=pltpu.VMEM((2, cols, rows), BF16),
        scratch_shapes=[pltpu.VMEM((2, rows - first.shape[1], cols), BF16), pltpu.SemaphoreType.DMA(())],
        compiler_params=PARAMS,
        cost_estimate=pl.CostEstimate(
            flops=8 * rows * size * cols, bytes_accessed=8 * rows * cols + 4 * rows * size, transcendentals=0
        ),
        name="left_focus",
    )(focusing, first, in_hbm(responses))


def slice_order(count):
    bits = count.bit_length() - 1
    return sorted(range(count), key=lambda e: tuple((e >> b) & 1 for b in range(bits)))


def weights_kernel(pieces, count, per_row, gathered, g_hbm, p_hbm, f_hbm, r_hbm, *rest):
    chunks = len(pieces)
    outs = rest[:chunks]
    f_out, r_out, g_ref, p_ref, scratch, sems, extra = rest[chunks:]
    me = lax.axis_index("col")
    here, size = g_ref.shape[1], g_ref.shape[2]
    first = me * here if gathered else lax.rem(me * here, per_row)
    width = p_ref.shape[2]
    part = width // count
    copies = []
    for j in range(here):
        rows = pl.ds(j * size, size)
        copies.append(
            (
                pltpu.make_async_copy(g_hbm.at[:, first + j], g_ref.at[:, j], sems.at[0, j]),
                pltpu.make_async_copy(p_hbm.at[:, rows, :], p_ref.at[:, rows, :], sems.at[1, j]),
            )
        )
        for copy in copies[-1]:
            copy.start()
    later = (
        pltpu.make_async_copy(f_hbm, f_out, extra.at[0]),
        pltpu.make_async_copy(r_hbm.at[:, pl.ds(0, r_out.shape[1]), :], r_out, extra.at[1]),
    )
    for copy in later:
        copy.start()
    for j in range(here):
        for copy in copies[j]:
            copy.wait()
        rows = pl.ds(j * size, size)
        p_re, p_im = p_ref[0, rows, :], p_ref[1, rows, :]
        left = jnp.concatenate([jnp.concatenate([p_re, p_im], 1), jnp.concatenate([p_im, -p_re], 1)], 0)
        right = jnp.concatenate([g_ref[0, j], g_ref[1, j]], 0)
        scratch[...] = mm(left, right, 0, 0).reshape(2, width, size)
        for at, e in enumerate(slice_order(count)):
            base = jnp.bitwise_xor(me, e) * part
            done = 0
            for i, piece in enumerate(pieces):
                start = pl.multiple_of(base + done, 8)
                outs[i][at, :, :, rows] = scratch[:, pl.ds(start, piece), :].astype(BF16)
                done += piece
    for copy in later:
        copy.wait()


def weights(blocks, panel, focusing, responses, pieces, count, per_row, gathered):
    size = blocks.shape[-1]
    _, cols, width = panel.shape
    here = cols // size
    _, rows, wide = responses.shape
    head = (rows // size + 1) // 2 * size
    return pl.pallas_call(
        functools.partial(weights_kernel, pieces, count, per_row, gathered),
        in_specs=[HBM] * 4,
        out_specs=[VMEM] * (len(pieces) + 2),
        out_shape=[pltpu.VMEM((count, 2, piece, cols), BF16) for piece in pieces]
        + [pltpu.VMEM(focusing.shape, BF16), pltpu.VMEM((2, head, wide), BF16)],
        scratch_shapes=[
            pltpu.VMEM((2, here, size, size), BF16),
            pltpu.VMEM((2, cols, width), BF16),
            pltpu.VMEM((2, width, size), F32),
            pltpu.SemaphoreType.DMA((2, here)),
            pltpu.SemaphoreType.DMA((2,)),
        ],
        compiler_params=PARAMS,
        cost_estimate=pl.CostEstimate(
            flops=8 * cols * size * width, bytes_accessed=4 * cols * (2 * width + size), transcendentals=0
        ),
        name="weights",
    )(in_hbm(blocks), in_hbm(panel), in_hbm(focusing), in_hbm(responses))


def product_kernel(own_row, own_ref, got_ref, left_ref, keep_ref, send_ref, full_ref):
    count, _, piece, cols = own_ref.shape
    h = own_ref[...]
    if own_row is not None:
        mine = lax.axis_index("row") == (lax.axis_index("col") * own_row[0]) // own_row[1]
        h = jnp.where(mine, h, got_ref[...])
    full_ref[:, :, :, :cols] = h
    full_ref[:, 0, :, cols:] = -h[:, 1]
    full_ref[:, 1, :, cols:] = h[:, 0]
    rows = left_ref.shape[2]
    tile = min(TILE, rows)
    half = count // 2

    @pl.loop(0, rows // tile)
    def _(t):
        at = pl.ds(pl.multiple_of(t * tile, tile), tile)
        left = jnp.concatenate([left_ref[0, :, at], left_ref[1, :, at]], 0)
        out = mm(full_ref[...].reshape(count * 2 * piece, 2 * cols), left, 1, 0)
        out = out.reshape(count, 2, piece, tile)
        keep_ref[:, :, :, at] = out[:half]
        send_ref[:, :, :, at] = out[half:].astype(send_ref.dtype)


def product(own, got, left, own_row):
    count, _, piece, cols = own.shape
    rows = left.shape[2]
    half = count // 2
    return pl.pallas_call(
        functools.partial(product_kernel, own_row),
        in_specs=[VMEM] * 3,
        out_specs=[VMEM] * 2,
        out_shape=[pltpu.VMEM((half, 2, piece, rows), F32), pltpu.VMEM((half, 2, piece, rows), FIRST)],
        scratch_shapes=[pltpu.VMEM((count, 2, piece, 2 * cols), BF16)],
        compiler_params=PARAMS,
        cost_estimate=pl.CostEstimate(
            flops=8 * count * piece * cols * rows,
            bytes_accessed=4 * rows * cols + 12 * half * piece * rows,
            transcendentals=0,
        ),
        name="product",
    )(own, in_vmem(got), left)


def swap(value, axis, bit):
    count = lax.axis_size(axis)
    return lax.ppermute(value, axis, [(i, i ^ bit) for i in range(count)])


def small(kernel, outs, *args):
    size = sum(a.size for a in args)
    return pl.pallas_call(
        kernel,
        in_specs=[VMEM] * len(args),
        out_specs=[VMEM] * len(outs),
        out_shape=[pltpu.VMEM(shape, kind) for shape, kind in outs],
        compiler_params=SMALL,
        cost_estimate=pl.CostEstimate(flops=size, bytes_accessed=4 * size, transcendentals=0),
    )(*[in_vmem(a) for a in args])


def halve_kernel(keep_ref, got_ref, on_ref, send_ref):
    half = on_ref.shape[0]
    on_ref[...] = keep_ref[:half] + got_ref[:half].astype(F32)
    send_ref[...] = (keep_ref[half:] + got_ref[half:].astype(F32)).astype(send_ref.dtype)


def part_kernel(keep_ref, got_ref, on_ref, send_ref):
    mine = jnp.bitwise_and(lax.axis_index("bin"), 1)
    other = 1 - mine
    on_ref[...] = keep_ref[0, mine] + got_ref[0, mine].astype(F32)
    send_ref[...] = (keep_ref[0, other] + got_ref[0, other].astype(F32)).astype(send_ref.dtype)


def settle_kernel(keep_ref, got_ref, o_ref):
    o_ref[...] = (keep_ref[0] + got_ref[0].astype(F32)).astype(o_ref.dtype)


def add_kernel(a_ref, b_ref, o_ref):
    o_ref[...] = (a_ref[...].astype(F32) + b_ref[...].astype(F32)).astype(o_ref.dtype)


def reduce_chunk(i, keep, send):
    count, bins = lax.axis_size("col"), lax.axis_size("bin")
    bit = 1
    while True:
        got = swap(send, "col", bit)
        bit *= 2
        if bit == count:
            break
        shape = (keep.shape[0] // 2,) + keep.shape[1:]
        keep, send = small(halve_kernel, [(shape, F32), (shape, BF16)], keep, got)
    if i in HALVED:
        return sum_by_halves(keep, got, bins)
    mine, bit = None, 1
    while bit < bins:
        kind = BF16 if bit * 4 >= bins else F32
        if mine is None:
            (mine,) = small(settle_kernel, [(keep.shape[1:], kind)], keep, got)
        else:
            (mine,) = small(add_kernel, [(mine.shape, kind)], mine, got)
        got = swap(mine, "bin", bit)
        bit *= 2
    return mine, got


def sum_by_halves(keep, got, bins):
    shape = keep.shape[2:]
    half, send = small(part_kernel, [(shape, F32), (shape, BF16)], keep, got)
    got = swap(send, "bin", 1)
    bit = 2
    while bit < bins:
        (half,) = small(add_kernel, [(shape, BF16 if bit * 2 == bins else F32)], half, got)
        got = swap(half, "bin", bit)
        bit *= 2
    (half,) = small(add_kernel, [(shape, BF16)], half, got)
    return half, swap(half, "bin", 1)


def write_kernel(chunks, first, *refs):
    values, out, held, sem = refs[: 2 * len(chunks)], refs[-3], refs[-2], refs[-1]
    here = jnp.bitwise_and(lax.axis_index("bin"), 1)
    done = 0
    for k, i in enumerate(chunks):
        mine, other = values[2 * k], values[2 * k + 1]
        rows = pl.ds(done, mine.shape[-2])
        if i in HALVED:
            held[here, rows, :] = mine[...].astype(F32)
            held[1 - here, rows, :] = other[...].astype(F32)
        else:
            held[:, rows, :] = mine[...].astype(F32) + other[...].astype(F32)
        done += mine.shape[-2]
    copy = pltpu.make_async_copy(held, out.at[:, pl.ds(first, done), :], sem)
    copy.start()
    copy.wait()


def write(chunks, first, parts, shape, before):
    values = [in_vmem(v) for i in chunks for v in parts[i]]
    rows = sum(parts[i][0].shape[-2] for i in chunks)
    kept = [] if before is None else [before]
    return pl.pallas_call(
        functools.partial(write_kernel, chunks, first),
        in_specs=[VMEM] * len(values) + [HBM] * len(kept),
        out_specs=HBM,
        out_shape=jax.ShapeDtypeStruct(shape, F32),
        scratch_shapes=[pltpu.VMEM((2, rows, shape[2]), F32), pltpu.SemaphoreType.DMA(())],
        input_output_aliases={len(values): 0} if kept else {},
        compiler_params=SMALL,
        name="write",
    )(*values, *kept)


def split_of(part):
    return [part * s // sum(SPLIT) for s in SPLIT]


def local(responses, focusing, panel):
    _, _, tile_rows, tile_cols = responses.shape
    per_row, size = focusing.shape[2], focusing.shape[3]
    here = tile_cols // size
    count = lax.axis_size("col")
    row_count = lax.axis_size("row")
    gathered = not (row_count == 2 and per_row % here == 0)
    pieces = split_of(panel.shape[2] // count)
    chunks = len(pieces)
    responses = responses.reshape(2, tile_rows, tile_cols)
    focusing = focusing.reshape(2, per_row, size, size)
    if gathered:
        blocks = lax.all_gather(focusing, "row", axis=1, tiled=True)
        *own, g_in, r_in = weights(blocks, panel, focusing, responses, pieces, count, per_row, True)
        got, own_row = own, None
    else:
        *own, g_in, r_in = weights(focusing, panel, focusing, responses, pieces, count, per_row, False)
        pairs = []
        for col in range(count):
            holder = (col * here) // per_row
            pairs.append((holder * count + col, (1 - holder) * count + col))
        got = []
        for i in range(chunks):
            got.append(lax.ppermute(own[i], ("row", "col"), pairs))
        own_row = (here, per_row)
    left = left_focus(g_in, r_in, responses)
    parts = []
    for i in range(chunks):
        keep, send = product(own[i], got[i], left, own_row)
        parts.append(reduce_chunk(i, keep, send))
    shape = (2, sum(pieces), tile_rows)
    out, head = None, chunks - 1
    if head:
        out = write(tuple(range(head)), 0, parts, shape, None)
    return write((head,), sum(pieces[:head]), parts, shape, out)


def solution(mesh):
    return jax.shard_map(
        local,
        mesh=mesh,
        in_specs=(
            P(None, "bin", "row", "col"),
            P(None, "bin", "row", None, None),
            P(None, "col", None),
        ),
        out_specs=P(None, "col", "row"),
        check_vma=False,
    )
```

profile of v0, /device:TPU:0, one launch (start us, length us, event | category | flops | bytes accessed | tf_op | source)
XLA Modules:
  0.0 70.0 jit_solution(5644342003604238222)
XLA Ops:
  0.0 3.6 %weights.1 = (bf16[4,2,16,1024]{3,2,1,0:T(8,128)(2,1)S(1)}, bf16[4,2,16,1024]{3,2,1,0:T(8,128)(2,1)S(1)}, bf16[4,2,16,1024]{3,2,1,0:T(8,128)(2,1)S(1)}, bf16[4,2...) custom-call(bf16[2,8,256,256]{3,2,1,0:T(8,128)(2,1)} %bitcast.4, ...), custom_call_target="tpu_custom_call" | custom-call | flops 536870912 | bytes 3145728 | tf_op jit(solution)/shard_map/weights/pallas_call | solution.py:128
  3.6 4.9 %collective-permute-start.18 = (bf16[4,2,16,1024]{3,2,1,0:T(8,128)(2,1)S(1)}, bf16[4,2,16,1024]{3,2,1,0:T(8,128)(2,1)S(1)}, u32[]{:S(2)}, u32[]{:S(2)}) collective-permute-start(bf16[4,2,16,1024]{3,2,1,0:T(8,128)(2,1)S(1)} %get-tuple-element.58.own_ref), channel_id=1, source_target_pairs={{0,4},{1,5},{6,2},{7,3},{8,12},{9,13},{14,10},{15,11},{16,20},{17,... | collective-permute-start | bytes 786440 | tf_op jit(solution)/shard_map/ppermute | solution.py:328
  8.5 1.3 %collective-permute-start.12 = (bf16[4,2,16,1024]{3,2,1,0:T(8,128)(2,1)S(1)}, bf16[4,2,16,1024]{3,2,1,0:T(8,128)(2,1)S(1)}, u32[]{:S(2)}, u32[]{:S(2)}) collective-permute-start(bf16[4,2,16,1024]{3,2,1,0:T(8,128)(2,1)S(1)} %get-tuple-element.51.own_ref), channel_id=1, source_target_pairs={{0,4},{1,5},{6,2},{7,3},{8,12},{9,13},{14,10},{15,11},{16,20},{17,... | collective-permute-start | bytes 786440 | tf_op jit(solution)/shard_map/ppermute | solution.py:328
  9.8 1.3 %collective-permute-start.6 = (bf16[4,2,16,1024]{3,2,1,0:T(8,128)(2,1)S(1)}, bf16[4,2,16,1024]{3,2,1,0:T(8,128)(2,1)S(1)}, u32[]{:S(2)}, u32[]{:S(2)}) collective-permute-start(bf16[4,2,16,1024]{3,2,1,0:T(8,128)(2,1)S(1)} %get-tuple-element.44.own_ref), channel_id=1, source_target_pairs={{0,4},{1,5},{6,2},{7,3},{8,12},{9,13},{14,10},{15,11},{16,20},{17,... | collective-permute-start | bytes 786440 | tf_op jit(solution)/shard_map/ppermute | solution.py:328
  12.4 5.0 %left_focus.1.left_ref = bf16[2,1024,2048]{2,1,0:T(8,128)(2,1)S(1)} custom-call(bf16[2,8,256,256]{3,2,1,0:T(8,128)(2,1)S(1)} %get-tuple-element.36.g_ref, bf16[2,1024,1024]{2,1,0:T(8,128)(2,1)S(1)} %get-tuple-element.37.first_ref, bf16[2,2048,1024]{2,1,0:T(8,128)(2,1)} %bitcast.3), custom_call_target="tpu_custom_call" | custom-call | flops 4294967296 | bytes 18874368 | tf_op jit(solution)/shard_map/left_focus/pallas_call | solution.py:58
  17.5 1.9 %product.7 = (f32[2,2,16,2048]{3,2,1,0:T(8,128)S(1)}, f32[2,2,16,2048]{3,2,1,0:T(8,128)S(1)}) custom-call(bf16[4,2,16,1024]{3,2,1,0:T(8,128)(2,1)S(1)} %get-tuple-element.58.own_ref, bf16[4,2,16,1024]{3,2,1,0:T(8,128)(2,1)S(1)} %collective-permute-done.18.got_ref, bf16[2,1024,2048]{2,1,0:T(8,128)(2,1)S(1)} %left_focus.1.left_ref), custom_call_target="tpu_custom_call" | custom-call | flops 1073741824 | bytes 9175040 | tf_op jit(solution)/shard_map/product/pallas_call | solution.py:176
  19.5 1.3 %collective-permute-done.12.got_ref = bf16[4,2,16,1024]{3,2,1,0:T(8,128)(2,1)S(1)} collective-permute-done((bf16[4,2,16,1024]{3,2,1,0:T(8,128)(2,1)S(1)}, bf16[4,2,16,1024]{3,2,1,0:T(8,128)(2,1)S(1)}, u32[]{:S(2)}, u32[]{:S(2)}) %collective-permute-start.12) | collective-permute-done | bytes 262176 | tf_op jit(solution)/shard_map/ppermute | solution.py:328
  20.8 1.9 %product.6 = (f32[2,2,16,2048]{3,2,1,0:T(8,128)S(1)}, f32[2,2,16,2048]{3,2,1,0:T(8,128)S(1)}) custom-call(bf16[4,2,16,1024]{3,2,1,0:T(8,128)(2,1)S(1)} %get-tuple-element.51.own_ref, bf16[4,2,16,1024]{3,2,1,0:T(8,128)(2,1)S(1)} %collective-permute-done.12.got_ref, bf16[2,1024,2048]{2,1,0:T(8,128)(2,1)S(1)} %left_focus.1.left_ref), custom_call_target="tpu_custom_call" | custom-call | flops 1073741824 | bytes 9175040 | tf_op jit(solution)/shard_map/product/pallas_call | solution.py:176
  22.7 3.7 %collective-permute-done.6.got_ref = bf16[4,2,16,1024]{3,2,1,0:T(8,128)(2,1)S(1)} collective-permute-done((bf16[4,2,16,1024]{3,2,1,0:T(8,128)(2,1)S(1)}, bf16[4,2,16,1024]{3,2,1,0:T(8,128)(2,1)S(1)}, u32[]{:S(2)}, u32[]{:S(2)}) %collective-permute-start.6) | collective-permute-done | bytes 262176 | tf_op jit(solution)/shard_map/ppermute | solution.py:328
  26.4 1.9 %product.5 = (f32[2,2,16,2048]{3,2,1,0:T(8,128)S(1)}, f32[2,2,16,2048]{3,2,1,0:T(8,128)S(1)}) custom-call(bf16[4,2,16,1024]{3,2,1,0:T(8,128)(2,1)S(1)} %get-tuple-element.44.own_ref, bf16[4,2,16,1024]{3,2,1,0:T(8,128)(2,1)S(1)} %collective-permute-done.6.got_ref, bf16[2,1024,2048]{2,1,0:T(8,128)(2,1)S(1)} %left_focus.1.left_ref), custom_call_target="tpu_custom_call" | custom-call | flops 1073741824 | bytes 9175040 | tf_op jit(solution)/shard_map/product/pallas_call | solution.py:176
  28.4 2.5 %collective-permute-done.got_ref = bf16[4,2,16,1024]{3,2,1,0:T(8,128)(2,1)S(1)} collective-permute-done((bf16[4,2,16,1024]{3,2,1,0:T(8,128)(2,1)S(1)}, bf16[4,2,16,1024]{3,2,1,0:T(8,128)(2,1)S(1)}, u32[]{:S(2)}, u32[]{:S(2)}) %collective-permute-start) | collective-permute-done | bytes 262176 | tf_op jit(solution)/shard_map/ppermute | solution.py:328
  30.9 1.9 %product.4 = (f32[2,2,16,2048]{3,2,1,0:T(8,128)S(1)}, f32[2,2,16,2048]{3,2,1,0:T(8,128)S(1)}) custom-call(bf16[4,2,16,1024]{3,2,1,0:T(8,128)(2,1)S(1)} %get-tuple-element.35.own_ref, bf16[4,2,16,1024]{3,2,1,0:T(8,128)(2,1)S(1)} %collective-permute-done.got_ref, bf16[2,1024,2048]{2,1,0:T(8,128)(2,1)S(1)} %left_focus.1.left_ref), custom_call_target="tpu_custom_call" | custom-call | flops 1073741824 | bytes 9175040 | tf_op jit(solution)/shard_map/product/pallas_call | solution.py:176
  32.9 2.5 %collective-permute-start.20 = (bf16[1,2,16,2048]{3,2,1,0:T(8,128)(2,1)S(1)}, bf16[1,2,16,2048]{3,2,1,0:T(8,128)(2,1)S(1)}, u32[]{:S(2)}, u32[]{:S(2)}) collective-permute-start(bf16[1,2,16,2048]{3,2,1,0:T(8,128)(2,1)S(1)} %get-tuple-element.62), channel_id=1, source_target_pairs={{0,2},{1,3},{2,0},{3,1},{4,6},{5,7},{6,4},{7,5},{8,10},{9,11},{10,... | collective-permute-start | bytes 393224 | tf_op jit(solution)/shard_map/ppermute | solution.py:194
  35.7 2.1 %collective-permute-start.8 = (bf16[1,2,16,2048]{3,2,1,0:T(8,128)(2,1)S(1)}, bf16[1,2,16,2048]{3,2,1,0:T(8,128)(2,1)S(1)}, u32[]{:S(2)}, u32[]{:S(2)}) collective-permute-start(bf16[1,2,16,2048]{3,2,1,0:T(8,128)(2,1)S(1)} %get-tuple-element.48), channel_id=1, source_target_pairs={{0,2},{1,3},{2,0},{3,1},{4,6},{5,7},{6,4},{7,5},{8,10},{9,11},{10,... | collective-permute-start | bytes 393224 | tf_op jit(solution)/shard_map/ppermute | solution.py:194
  37.9 1.9 %collective-permute-done.20.got_ref = bf16[1,2,16,2048]{3,2,1,0:T(8,128)(2,1)S(1)} collective-permute-done((bf16[1,2,16,2048]{3,2,1,0:T(8,128)(2,1)S(1)}, bf16[1,2,16,2048]{3,2,1,0:T(8,128)(2,1)S(1)}, u32[]{:S(2)}, u32[]{:S(2)}) %collective-permute-start.20) | collective-permute-done | bytes 131104 | tf_op jit(solution)/shard_map/ppermute | solution.py:194
  39.8 1.6 %collective-permute-start.21 = (bf16[16,2048]{1,0:T(8,128)(2,1)S(1)}, bf16[16,2048]{1,0:T(8,128)(2,1)S(1)}, u32[]{:S(2)}, u32[]{:S(2)}) collective-permute-start(bf16[16,2048]{1,0:T(8,128)(2,1)S(1)} %get-tuple-element.64), channel_id=1, source_target_pairs={{0,8},{8,0},{16,24},{24,16},{1,9},{9,1},{17,25},{25,17},{2,10},{10... | collective-permute-start | bytes 196616 | tf_op jit(solution)/shard_map/ppermute | solution.py:194
  42.6 1.6 %collective-permute-start.15 = (bf16[16,2048]{1,0:T(8,128)(2,1)S(1)}, bf16[16,2048]{1,0:T(8,128)(2,1)S(1)}, u32[]{:S(2)}, u32[]{:S(2)}) collective-permute-start(bf16[16,2048]{1,0:T(8,128)(2,1)S(1)} %get-tuple-element.57), channel_id=1, source_target_pairs={{0,8},{8,0},{16,24},{24,16},{1,9},{9,1},{17,25},{25,17},{2,10},{10... | collective-permute-start | bytes 196616 | tf_op jit(solution)/shard_map/ppermute | solution.py:194
  45.4 1.6 %collective-permute-start.9 = (bf16[16,2048]{1,0:T(8,128)(2,1)S(1)}, bf16[16,2048]{1,0:T(8,128)(2,1)S(1)}, u32[]{:S(2)}, u32[]{:S(2)}) collective-permute-start(bf16[16,2048]{1,0:T(8,128)(2,1)S(1)} %get-tuple-element.50), channel_id=1, source_target_pairs={{0,8},{8,0},{16,24},{24,16},{1,9},{9,1},{17,25},{25,17},{2,10},{10... | collective-permute-start | bytes 196616 | tf_op jit(solution)/shard_map/ppermute | solution.py:194
  48.1 1.6 %collective-permute-start.3 = (bf16[16,2048]{1,0:T(8,128)(2,1)S(1)}, bf16[16,2048]{1,0:T(8,128)(2,1)S(1)}, u32[]{:S(2)}, u32[]{:S(2)}) collective-permute-start(bf16[16,2048]{1,0:T(8,128)(2,1)S(1)} %get-tuple-element.43), channel_id=1, source_target_pairs={{0,8},{8,0},{16,24},{24,16},{1,9},{9,1},{17,25},{25,17},{2,10},{10... | collective-permute-start | bytes 196616 | tf_op jit(solution)/shard_map/ppermute | solution.py:194
  49.7 2.6 %collective-permute-start.22 = (bf16[16,2048]{1,0:T(8,128)(2,1)S(1)}, bf16[16,2048]{1,0:T(8,128)(2,1)S(1)}, u32[]{:S(2)}, u32[]{:S(2)}) collective-permute-start(bf16[16,2048]{1,0:T(8,128)(2,1)S(1)} %shard_map.51.a_ref), channel_id=1, source_target_pairs={{0,16},{8,24},{16,0},{24,8},{1,17},{9,25},{17,1},{25,9},{2,18},{10... | collective-permute-start | bytes 196616 | tf_op jit(solution)/shard_map/ppermute | solution.py:194
  52.8 2.6 %collective-permute-start.10 = (bf16[16,2048]{1,0:T(8,128)(2,1)S(1)}, bf16[16,2048]{1,0:T(8,128)(2,1)S(1)}, u32[]{:S(2)}, u32[]{:S(2)}) collective-permute-start(bf16[16,2048]{1,0:T(8,128)(2,1)S(1)} %shard_map.43.a_ref), channel_id=1, source_target_pairs={{0,16},{8,24},{16,0},{24,8},{1,17},{9,25},{17,1},{25,9},{2,18},{10... | collective-permute-start | bytes 196616 | tf_op jit(solution)/shard_map/ppermute | solution.py:194
  55.9 3.6 %collective-permute-done.22.b_ref = bf16[16,2048]{1,0:T(8,128)(2,1)S(1)} collective-permute-done((bf16[16,2048]{1,0:T(8,128)(2,1)S(1)}, bf16[16,2048]{1,0:T(8,128)(2,1)S(1)}, u32[]{:S(2)}, u32[]{:S(2)}) %collective-permute-start.22) | collective-permute-done | bytes 65568 | tf_op jit(solution)/shard_map/ppermute | solution.py:194
  65.5 1.4 %collective-permute-done.17.refs_3_ = bf16[16,2048]{1,0:T(8,128)(2,1)S(1)} collective-permute-done((bf16[16,2048]{1,0:T(8,128)(2,1)S(1)}, bf16[16,2048]{1,0:T(8,128)(2,1)S(1)}, u32[]{:S(2)}, u32[]{:S(2)}) %collective-permute-start.17) | collective-permute-done | bytes 65568 | tf_op jit(solution)/shard_map/ppermute | solution.py:194
  66.9 1.4 %collective-permute-done.11.refs_1_ = bf16[16,2048]{1,0:T(8,128)(2,1)S(1)} collective-permute-done((bf16[16,2048]{1,0:T(8,128)(2,1)S(1)}, bf16[16,2048]{1,0:T(8,128)(2,1)S(1)}, u32[]{:S(2)}, u32[]{:S(2)}) %collective-permute-start.11) | collective-permute-done | bytes 65568 | tf_op jit(solution)/shard_map/ppermute | solution.py:194
  (48 shorter events, 13.9 us)
Async XLA Ops:
  3.6 13.9 %collective-permute-start.18 = (bf16[4,2,16,1024]{3,2,1,0:T(8,128)(2,1)S(1)}, bf16[4,2,16,1024]{3,2,1,0:T(8,128)(2,1)S(1)}, u32[]{:S(2)}, u32[]{:S(2)}) collective-permute-start(bf16[4,2,16,1024]{3,2,1,0:T(8,128)(2,1)S(1)} %get-tuple-element.58.own_ref), channel_id=1, source_target_pairs={{0,4},{1,5},{6,2},{7,3},{8,12},{9,13},{14,10},{15,11},{16,20},{17,... | collective-permute-start | bytes 786440 | tf_op jit(solution)/shard_map/ppermute | solution.py:328
  8.5 12.3 %collective-permute-start.12 = (bf16[4,2,16,1024]{3,2,1,0:T(8,128)(2,1)S(1)}, bf16[4,2,16,1024]{3,2,1,0:T(8,128)(2,1)S(1)}, u32[]{:S(2)}, u32[]{:S(2)}) collective-permute-start(bf16[4,2,16,1024]{3,2,1,0:T(8,128)(2,1)S(1)} %get-tuple-element.51.own_ref), channel_id=1, source_target_pairs={{0,4},{1,5},{6,2},{7,3},{8,12},{9,13},{14,10},{15,11},{16,20},{17,... | collective-permute-start | bytes 786440 | tf_op jit(solution)/shard_map/ppermute | solution.py:328
  9.8 16.6 %collective-permute-start.6 = (bf16[4,2,16,1024]{3,2,1,0:T(8,128)(2,1)S(1)}, bf16[4,2,16,1024]{3,2,1,0:T(8,128)(2,1)S(1)}, u32[]{:S(2)}, u32[]{:S(2)}) collective-permute-start(bf16[4,2,16,1024]{3,2,1,0:T(8,128)(2,1)S(1)} %get-tuple-element.44.own_ref), channel_id=1, source_target_pairs={{0,4},{1,5},{6,2},{7,3},{8,12},{9,13},{14,10},{15,11},{16,20},{17,... | collective-permute-start | bytes 786440 | tf_op jit(solution)/shard_map/ppermute | solution.py:328
  11.1 19.8 %collective-permute-start = (bf16[4,2,16,1024]{3,2,1,0:T(8,128)(2,1)S(1)}, bf16[4,2,16,1024]{3,2,1,0:T(8,128)(2,1)S(1)}, u32[]{:S(2)}, u32[]{:S(2)}) collective-permute-start(bf16[4,2,16,1024]{3,2,1,0:T(8,128)(2,1)S(1)} %get-tuple-element.35.own_ref), channel_id=1, source_target_pairs={{0,4},{1,5},{6,2},{7,3},{8,12},{9,13},{14,10},{15,11},{16,20},{17,... | collective-permute-start | bytes 786440 | tf_op jit(solution)/shard_map/ppermute | solution.py:328
  19.4 13.5 %collective-permute-start.19 = (f32[2,2,16,2048]{3,2,1,0:T(8,128)S(1)}, f32[2,2,16,2048]{3,2,1,0:T(8,128)S(1)}, u32[]{:S(2)}, u32[]{:S(2)}) collective-permute-start(f32[2,2,16,2048]{3,2,1,0:T(8,128)S(1)} %get-tuple-element.60), channel_id=1, source_target_pairs={{0,1},{1,0},{2,3},{3,2},{4,5},{5,4},{6,7},{7,6},{8,9},{9,8},{10,11... | collective-permute-start | bytes 1572872 | tf_op jit(solution)/shard_map/ppermute | solution.py:194
  22.7 12.8 %collective-permute-start.13 = (f32[2,2,16,2048]{3,2,1,0:T(8,128)S(1)}, f32[2,2,16,2048]{3,2,1,0:T(8,128)S(1)}, u32[]{:S(2)}, u32[]{:S(2)}) collective-permute-start(f32[2,2,16,2048]{3,2,1,0:T(8,128)S(1)} %get-tuple-element.53), channel_id=1, source_target_pairs={{0,1},{1,0},{2,3},{3,2},{4,5},{5,4},{6,7},{7,6},{8,9},{9,8},{10,11... | collective-permute-start | bytes 1572872 | tf_op jit(solution)/shard_map/ppermute | solution.py:194
  28.3 7.3 %collective-permute-start.7 = (f32[2,2,16,2048]{3,2,1,0:T(8,128)S(1)}, f32[2,2,16,2048]{3,2,1,0:T(8,128)S(1)}, u32[]{:S(2)}, u32[]{:S(2)}) collective-permute-start(f32[2,2,16,2048]{3,2,1,0:T(8,128)S(1)} %get-tuple-element.46), channel_id=1, source_target_pairs={{0,1},{1,0},{2,3},{3,2},{4,5},{5,4},{6,7},{7,6},{8,9},{9,8},{10,11... | collective-permute-start | bytes 1572872 | tf_op jit(solution)/shard_map/ppermute | solution.py:194
  32.8 5.0 %collective-permute-start.1 = (f32[2,2,16,2048]{3,2,1,0:T(8,128)S(1)}, f32[2,2,16,2048]{3,2,1,0:T(8,128)S(1)}, u32[]{:S(2)}, u32[]{:S(2)}) collective-permute-start(f32[2,2,16,2048]{3,2,1,0:T(8,128)S(1)} %get-tuple-element.39), channel_id=1, source_target_pairs={{0,1},{1,0},{2,3},{3,2},{4,5},{5,4},{6,7},{7,6},{8,9},{9,8},{10,11... | collective-permute-start | bytes 1572872 | tf_op jit(solution)/shard_map/ppermute | solution.py:194
  32.9 6.9 %collective-permute-start.20 = (bf16[1,2,16,2048]{3,2,1,0:T(8,128)(2,1)S(1)}, bf16[1,2,16,2048]{3,2,1,0:T(8,128)(2,1)S(1)}, u32[]{:S(2)}, u32[]{:S(2)}) collective-permute-start(bf16[1,2,16,2048]{3,2,1,0:T(8,128)(2,1)S(1)} %get-tuple-element.62), channel_id=1, source_target_pairs={{0,2},{1,3},{2,0},{3,1},{4,6},{5,7},{6,4},{7,5},{8,10},{9,11},{10,... | collective-permute-start | bytes 393224 | tf_op jit(solution)/shard_map/ppermute | solution.py:194
  35.5 7.1 %collective-permute-start.14 = (bf16[1,2,16,2048]{3,2,1,0:T(8,128)(2,1)S(1)}, bf16[1,2,16,2048]{3,2,1,0:T(8,128)(2,1)S(1)}, u32[]{:S(2)}, u32[]{:S(2)}) collective-permute-start(bf16[1,2,16,2048]{3,2,1,0:T(8,128)(2,1)S(1)} %get-tuple-element.55), channel_id=1, source_target_pairs={{0,2},{1,3},{2,0},{3,1},{4,6},{5,7},{6,4},{7,5},{8,10},{9,11},{10,... | collective-permute-start | bytes 393224 | tf_op jit(solution)/shard_map/ppermute | solution.py:194
  35.7 9.8 %collective-permute-start.8 = (bf16[1,2,16,2048]{3,2,1,0:T(8,128)(2,1)S(1)}, bf16[1,2,16,2048]{3,2,1,0:T(8,128)(2,1)S(1)}, u32[]{:S(2)}, u32[]{:S(2)}) collective-permute-start(bf16[1,2,16,2048]{3,2,1,0:T(8,128)(2,1)S(1)} %get-tuple-element.48), channel_id=1, source_target_pairs={{0,2},{1,3},{2,0},{3,1},{4,6},{5,7},{6,4},{7,5},{8,10},{9,11},{10,... | collective-permute-start | bytes 393224 | tf_op jit(solution)/shard_map/ppermute | solution.py:194
  37.8 10.2 %collective-permute-start.2 = (bf16[1,2,16,2048]{3,2,1,0:T(8,128)(2,1)S(1)}, bf16[1,2,16,2048]{3,2,1,0:T(8,128)(2,1)S(1)}, u32[]{:S(2)}, u32[]{:S(2)}) collective-permute-start(bf16[1,2,16,2048]{3,2,1,0:T(8,128)(2,1)S(1)} %get-tuple-element.41), channel_id=1, source_target_pairs={{0,2},{1,3},{2,0},{3,1},{4,6},{5,7},{6,4},{7,5},{8,10},{9,11},{10,... | collective-permute-start | bytes 393224 | tf_op jit(solution)/shard_map/ppermute | solution.py:194
  39.8 9.9 %collective-permute-start.21 = (bf16[16,2048]{1,0:T(8,128)(2,1)S(1)}, bf16[16,2048]{1,0:T(8,128)(2,1)S(1)}, u32[]{:S(2)}, u32[]{:S(2)}) collective-permute-start(bf16[16,2048]{1,0:T(8,128)(2,1)S(1)} %get-tuple-element.64), channel_id=1, source_target_pairs={{0,8},{8,0},{16,24},{24,16},{1,9},{9,1},{17,25},{25,17},{2,10},{10... | collective-permute-start | bytes 196616 | tf_op jit(solution)/shard_map/ppermute | solution.py:194
  42.6 9.7 %collective-permute-start.15 = (bf16[16,2048]{1,0:T(8,128)(2,1)S(1)}, bf16[16,2048]{1,0:T(8,128)(2,1)S(1)}, u32[]{:S(2)}, u32[]{:S(2)}) collective-permute-start(bf16[16,2048]{1,0:T(8,128)(2,1)S(1)} %get-tuple-element.57), channel_id=1, source_target_pairs={{0,8},{8,0},{16,24},{24,16},{1,9},{9,1},{17,25},{25,17},{2,10},{10... | collective-permute-start | bytes 196616 | tf_op jit(solution)/shard_map/ppermute | solution.py:194
  45.4 7.3 %collective-permute-start.9 = (bf16[16,2048]{1,0:T(8,128)(2,1)S(1)}, bf16[16,2048]{1,0:T(8,128)(2,1)S(1)}, u32[]{:S(2)}, u32[]{:S(2)}) collective-permute-start(bf16[16,2048]{1,0:T(8,128)(2,1)S(1)} %get-tuple-element.50), channel_id=1, source_target_pairs={{0,8},{8,0},{16,24},{24,16},{1,9},{9,1},{17,25},{25,17},{2,10},{10... | collective-permute-start | bytes 196616 | tf_op jit(solution)/shard_map/ppermute | solution.py:194
  48.1 7.4 %collective-permute-start.3 = (bf16[16,2048]{1,0:T(8,128)(2,1)S(1)}, bf16[16,2048]{1,0:T(8,128)(2,1)S(1)}, u32[]{:S(2)}, u32[]{:S(2)}) collective-permute-start(bf16[16,2048]{1,0:T(8,128)(2,1)S(1)} %get-tuple-element.43), channel_id=1, source_target_pairs={{0,8},{8,0},{16,24},{24,16},{1,9},{9,1},{17,25},{25,17},{2,10},{10... | collective-permute-start | bytes 196616 | tf_op jit(solution)/shard_map/ppermute | solution.py:194
  49.7 9.8 %collective-permute-start.22 = (bf16[16,2048]{1,0:T(8,128)(2,1)S(1)}, bf16[16,2048]{1,0:T(8,128)(2,1)S(1)}, u32[]{:S(2)}, u32[]{:S(2)}) collective-permute-start(bf16[16,2048]{1,0:T(8,128)(2,1)S(1)} %shard_map.51.a_ref), channel_id=1, source_target_pairs={{0,16},{8,24},{16,0},{24,8},{1,17},{9,25},{17,1},{25,9},{2,18},{10... | collective-permute-start | bytes 196616 | tf_op jit(solution)/shard_map/ppermute | solution.py:194
  52.4 9.2 %collective-permute-start.16 = (bf16[16,2048]{1,0:T(8,128)(2,1)S(1)}, bf16[16,2048]{1,0:T(8,128)(2,1)S(1)}, u32[]{:S(2)}, u32[]{:S(2)}) collective-permute-start(bf16[16,2048]{1,0:T(8,128)(2,1)S(1)} %shard_map.47.a_ref), channel_id=1, source_target_pairs={{0,16},{8,24},{16,0},{24,8},{1,17},{9,25},{17,1},{25,9},{2,18},{10... | collective-permute-start | bytes 196616 | tf_op jit(solution)/shard_map/ppermute | solution.py:194
  52.8 10.2 %collective-permute-start.10 = (bf16[16,2048]{1,0:T(8,128)(2,1)S(1)}, bf16[16,2048]{1,0:T(8,128)(2,1)S(1)}, u32[]{:S(2)}, u32[]{:S(2)}) collective-permute-start(bf16[16,2048]{1,0:T(8,128)(2,1)S(1)} %shard_map.43.a_ref), channel_id=1, source_target_pairs={{0,16},{8,24},{16,0},{24,8},{1,17},{9,25},{17,1},{25,9},{2,18},{10... | collective-permute-start | bytes 196616 | tf_op jit(solution)/shard_map/ppermute | solution.py:194
  55.5 8.8 %collective-permute-start.4 = (bf16[16,2048]{1,0:T(8,128)(2,1)S(1)}, bf16[16,2048]{1,0:T(8,128)(2,1)S(1)}, u32[]{:S(2)}, u32[]{:S(2)}) collective-permute-start(bf16[16,2048]{1,0:T(8,128)(2,1)S(1)} %shard_map.39.a_ref), channel_id=1, source_target_pairs={{0,16},{8,24},{16,0},{24,8},{1,17},{9,25},{17,1},{25,9},{2,18},{10... | collective-permute-start | bytes 196616 | tf_op jit(solution)/shard_map/ppermute | solution.py:194
  59.5 6.0 %collective-permute-start.23 = (bf16[16,2048]{1,0:T(8,128)(2,1)S(1)}, bf16[16,2048]{1,0:T(8,128)(2,1)S(1)}, u32[]{:S(2)}, u32[]{:S(2)}) collective-permute-start(bf16[16,2048]{1,0:T(8,128)(2,1)S(1)} %shard_map.52.refs_4_), channel_id=1, source_target_pairs={{0,8},{8,0},{16,24},{24,16},{1,9},{9,1},{17,25},{25,17},{2,10},{10... | collective-permute-start | bytes 196616 | tf_op jit(solution)/shard_map/ppermute | solution.py:194
  61.6 5.3 %collective-permute-start.17 = (bf16[16,2048]{1,0:T(8,128)(2,1)S(1)}, bf16[16,2048]{1,0:T(8,128)(2,1)S(1)}, u32[]{:S(2)}, u32[]{:S(2)}) collective-permute-start(bf16[16,2048]{1,0:T(8,128)(2,1)S(1)} %shard_map.48.refs_2_), channel_id=1, source_target_pairs={{0,8},{8,0},{16,24},{24,16},{1,9},{9,1},{17,25},{25,17},{2,10},{10... | collective-permute-start | bytes 196616 | tf_op jit(solution)/shard_map/ppermute | solution.py:194
  63.0 5.3 %collective-permute-start.11 = (bf16[16,2048]{1,0:T(8,128)(2,1)S(1)}, bf16[16,2048]{1,0:T(8,128)(2,1)S(1)}, u32[]{:S(2)}, u32[]{:S(2)}) collective-permute-start(bf16[16,2048]{1,0:T(8,128)(2,1)S(1)} %shard_map.44.refs_0_), channel_id=1, source_target_pairs={{0,8},{8,0},{16,24},{24,16},{1,9},{9,1},{17,25},{25,17},{2,10},{10... | collective-permute-start | bytes 196616 | tf_op jit(solution)/shard_map/ppermute | solution.py:194
  64.3 5.0 %collective-permute-start.5 = (bf16[16,2048]{1,0:T(8,128)(2,1)S(1)}, bf16[16,2048]{1,0:T(8,128)(2,1)S(1)}, u32[]{:S(2)}, u32[]{:S(2)}) collective-permute-start(bf16[16,2048]{1,0:T(8,128)(2,1)S(1)} %shard_map.40.refs_0_), channel_id=1, source_target_pairs={{0,8},{8,0},{16,24},{24,16},{1,9},{9,1},{17,25},{25,17},{2,10},{10... | collective-permute-start | bytes 196616 | tf_op jit(solution)/shard_map/ppermute | solution.py:194
where the time goes:
time: 70.2 us; the launch traced here: 70 us
  starting transfers between devices  29.9 us (43%)
  waiting for transfers between devices  21.6 us (31%)
  Pallas kernels  18.2 us (26%)
    ppermute x20, starting transfers between devices, swap(): return lax.ppermute(value, axis, [(i, i ^ bit) for i in range(count)])  21.1 us
    ppermute x20, waiting for transfers between devices, swap(): return lax.ppermute(value, axis, [(i, i ^ bit) for i in range(count)])  14.1 us
    ppermute x4, starting transfers between devices, local(): got.append(lax.ppermute(own[i], ('row', 'col'), pairs))  8.83 us
    pallas_call x4, Pallas kernels, product(): pl.pallas_call(functools.partial(product_kernel, own_row), in_specs=[VMEM...  7.53 us
    ppermute x4, waiting for transfers between devices, local(): got.append(lax.ppermute(own[i], ('row', 'col'), pairs))  7.49 us
    pallas_call x1, Pallas kernels, left_focus(): pl.pallas_call(left_kernel, in_specs=[VMEM, VMEM, HBM], out_specs=VMEM, o...  5.02 us
    pallas_call x1, Pallas kernels, weights(): pl.pallas_call(functools.partial(weights_kernel, pieces, count, per_row,...  3.57 us
    pallas_call x2, Pallas kernels, write(): pl.pallas_call(functools.partial(write_kernel, chunks, first), in_specs=[...  1.69 us
  transfers between devices with their start and end apart: 24, of which 14 were waited for; matrix products, arithmetic and copies ran while one was open for 0% of the time, Pallas kernels for 20%

commit v1 on v0

--- a/solution.py
+++ b/solution.py
@@ -9,6 +9,7 @@
 
 
 SPLIT = (1, 1, 1, 1)
+PARTS = (1, 1, 1, 1)
 HALVED = (0, 1, 2, 3)
 TILE = 512
 BF16, F32 = jnp.bfloat16, jnp.float32
@@ -146,7 +147,8 @@
     )(in_hbm(blocks), in_hbm(panel), in_hbm(focusing), in_hbm(responses))
 
 
-def product_kernel(own_row, own_ref, got_ref, left_ref, keep_ref, send_ref, full_ref):
+def product_kernel(own_row, parts, own_ref, got_ref, left_ref, *rest):
+    outs, full_ref = rest[:-1], rest[-1]
     count, _, piece, cols = own_ref.shape
     h = own_ref[...]
     if own_row is not None:
@@ -165,19 +167,22 @@
         left = jnp.concatenate([left_ref[0, :, at], left_ref[1, :, at]], 0)
         out = mm(full_ref[...].reshape(count * 2 * piece, 2 * cols), left, 1, 0)
         out = out.reshape(count, 2, piece, tile)
-        keep_ref[:, :, :, at] = out[:half]
-        send_ref[:, :, :, at] = out[half:].astype(send_ref.dtype)
-
-
-def product(own, got, left, own_row):
+        size = piece // parts
+        for k in range(parts):
+            keep_ref, send_ref = outs[2 * k], outs[2 * k + 1]
+            keep_ref[:, :, :, at] = out[:half, :, k * size : (k + 1) * size]
+            send_ref[:, :, :, at] = out[half:, :, k * size : (k + 1) * size].astype(send_ref.dtype)
+
+
+def product(own, got, left, own_row, parts):
     count, _, piece, cols = own.shape
     rows = left.shape[2]
     half = count // 2
     return pl.pallas_call(
-        functools.partial(product_kernel, own_row),
+        functools.partial(product_kernel, own_row, parts),
         in_specs=[VMEM] * 3,
-        out_specs=[VMEM] * 2,
-        out_shape=[pltpu.VMEM((half, 2, piece, rows), F32), pltpu.VMEM((half, 2, piece, rows), FIRST)],
+        out_specs=[VMEM] * (2 * parts),
+        out_shape=[pltpu.VMEM((half, 2, piece // parts, rows), kind) for kind in (F32, FIRST) * parts],
         scratch_shapes=[pltpu.VMEM((count, 2, piece, 2 * cols), BF16)],
         compiler_params=PARAMS,
         cost_estimate=pl.CostEstimate(
@@ -330,13 +335,14 @@
     left = left_focus(g_in, r_in, responses)
     parts = []
     for i in range(chunks):
-        keep, send = product(own[i], got[i], left, own_row)
-        parts.append(reduce_chunk(i, keep, send))
+        made = product(own[i], got[i], left, own_row, PARTS[i])
+        for k in range(PARTS[i]):
+            parts.append(reduce_chunk(len(parts), made[2 * k], made[2 * k + 1]))
     shape = (2, sum(pieces), tile_rows)
-    out, head = None, chunks - 1
+    out, head = None, len(parts) - 1
     if head:
         out = write(tuple(range(head)), 0, parts, shape, None)
-    return write((head,), sum(pieces[:head]), parts, shape, out)
+    return write((head,), shape[1] - parts[head][0].shape[-2], parts, shape, out)
 
 
 def solution(mesh):

time: 70.2 us -> 70.2 us (level)
  no operation moved by 1% of the time
where the time goes in v1:
time: 70.2 us; the launch traced here: 70 us
  starting transfers between devices  29.9 us (43%)
  waiting for transfers between devices  21.6 us (31%)
  Pallas kernels  18.2 us (26%)
    ppermute x20, starting transfers between devices, swap(): return lax.ppermute(value, axis, [(i, i ^ bit) for i in range(count)])  21.1 us
    ppermute x20, waiting for transfers between devices, swap(): return lax.ppermute(value, axis, [(i, i ^ bit) for i in range(count)])  14.1 us
    ppermute x4, starting transfers between devices, local(): got.append(lax.ppermute(own[i], ('row', 'col'), pairs))  8.83 us
    pallas_call x4, Pallas kernels, product(): pl.pallas_call(functools.partial(product_kernel, own_row, parts), in_spec...  7.53 us
    ppermute x4, waiting for transfers between devices, local(): got.append(lax.ppermute(own[i], ('row', 'col'), pairs))  7.49 us
    pallas_call x1, Pallas kernels, left_focus(): pl.pallas_call(left_kernel, in_specs=[VMEM, VMEM, HBM], out_specs=VMEM, o...  5.02 us
    pallas_call x1, Pallas kernels, weights(): pl.pallas_call(functools.partial(weights_kernel, pieces, count, per_row,...  3.57 us
    pallas_call x2, Pallas kernels, write(): pl.pallas_call(functools.partial(write_kernel, chunks, first), in_specs=[...  1.69 us
  transfers between devices with their start and end apart: 24, of which 14 were waited for; matrix products, arithmetic and copies ran while one was open for 0% of the time, Pallas kernels for 20%

profile of v1, /device:TPU:0, one launch (start us, length us, event | category | flops | bytes accessed | tf_op | source)
XLA Modules:
  0.0 70.0 jit_solution(5644342003604238222)
XLA Ops:
  0.0 3.6 %weights.1 = (bf16[4,2,16,1024]{3,2,1,0:T(8,128)(2,1)S(1)}, bf16[4,2,16,1024]{3,2,1,0:T(8,128)(2,1)S(1)}, bf16[4,2,16,1024]{3,2,1,0:T(8,128)(2,1)S(1)}, bf16[4,2...) custom-call(bf16[2,8,256,256]{3,2,1,0:T(8,128)(2,1)} %bitcast.4, ...), custom_call_target="tpu_custom_call" | custom-call | flops 536870912 | bytes 3145728 | tf_op jit(solution)/shard_map/weights/pallas_call | solution.py:129
  3.6 4.9 %collective-permute-start.18 = (bf16[4,2,16,1024]{3,2,1,0:T(8,128)(2,1)S(1)}, bf16[4,2,16,1024]{3,2,1,0:T(8,128)(2,1)S(1)}, u32[]{:S(2)}, u32[]{:S(2)}) collective-permute-start(bf16[4,2,16,1024]{3,2,1,0:T(8,128)(2,1)S(1)} %get-tuple-element.58.own_ref), channel_id=1, source_target_pairs={{0,4},{1,5},{6,2},{7,3},{8,12},{9,13},{14,10},{15,11},{16,20},{17,... | collective-permute-start | bytes 786440 | tf_op jit(solution)/shard_map/ppermute | solution.py:333
  8.5 1.3 %collective-permute-start.12 = (bf16[4,2,16,1024]{3,2,1,0:T(8,128)(2,1)S(1)}, bf16[4,2,16,1024]{3,2,1,0:T(8,128)(2,1)S(1)}, u32[]{:S(2)}, u32[]{:S(2)}) collective-permute-start(bf16[4,2,16,1024]{3,2,1,0:T(8,128)(2,1)S(1)} %get-tuple-element.51.own_ref), channel_id=1, source_target_pairs={{0,4},{1,5},{6,2},{7,3},{8,12},{9,13},{14,10},{15,11},{16,20},{17,... | collective-permute-start | bytes 786440 | tf_op jit(solution)/shard_map/ppermute | solution.py:333
  9.8 1.3 %collective-permute-start.6 = (bf16[4,2,16,1024]{3,2,1,0:T(8,128)(2,1)S(1)}, bf16[4,2,16,1024]{3,2,1,0:T(8,128)(2,1)S(1)}, u32[]{:S(2)}, u32[]{:S(2)}) collective-permute-start(bf16[4,2,16,1024]{3,2,1,0:T(8,128)(2,1)S(1)} %get-tuple-element.44.own_ref), channel_id=1, source_target_pairs={{0,4},{1,5},{6,2},{7,3},{8,12},{9,13},{14,10},{15,11},{16,20},{17,... | collective-permute-start | bytes 786440 | tf_op jit(solution)/shard_map/ppermute | solution.py:333
  12.4 5.0 %left_focus.1.left_ref = bf16[2,1024,2048]{2,1,0:T(8,128)(2,1)S(1)} custom-call(bf16[2,8,256,256]{3,2,1,0:T(8,128)(2,1)S(1)} %get-tuple-element.36.g_ref, bf16[2,1024,1024]{2,1,0:T(8,128)(2,1)S(1)} %get-tuple-element.37.first_ref, bf16[2,2048,1024]{2,1,0:T(8,128)(2,1)} %bitcast.3), custom_call_target="tpu_custom_call" | custom-call | flops 4294967296 | bytes 18874368 | tf_op jit(solution)/shard_map/left_focus/pallas_call | solution.py:59
  17.5 1.9 %product.7 = (f32[2,2,16,2048]{3,2,1,0:T(8,128)S(1)}, f32[2,2,16,2048]{3,2,1,0:T(8,128)S(1)}) custom-call(bf16[4,2,16,1024]{3,2,1,0:T(8,128)(2,1)S(1)} %get-tuple-element.58.own_ref, bf16[4,2,16,1024]{3,2,1,0:T(8,128)(2,1)S(1)} %collective-permute-done.18.got_ref, bf16[2,1024,2048]{2,1,0:T(8,128)(2,1)S(1)} %left_focus.1.left_ref), custom_call_target="tpu_custom_call" | custom-call | flops 1073741824 | bytes 9175040 | tf_op jit(solution)/shard_map/product/pallas_call | solution.py:181
  19.5 1.3 %collective-permute-done.12.got_ref = bf16[4,2,16,1024]{3,2,1,0:T(8,128)(2,1)S(1)} collective-permute-done((bf16[4,2,16,1024]{3,2,1,0:T(8,128)(2,1)S(1)}, bf16[4,2,16,1024]{3,2,1,0:T(8,128)(2,1)S(1)}, u32[]{:S(2)}, u32[]{:S(2)}) %collective-permute-start.12) | collective-permute-done | bytes 262176 | tf_op jit(solution)/shard_map/ppermute | solution.py:333
  20.8 1.9 %product.6 = (f32[2,2,16,2048]{3,2,1,0:T(8,128)S(1)}, f32[2,2,16,2048]{3,2,1,0:T(8,128)S(1)}) custom-call(bf16[4,2,16,1024]{3,2,1,0:T(8,128)(2,1)S(1)} %get-tuple-element.51.own_ref, bf16[4,2,16,1024]{3,2,1,0:T(8,128)(2,1)S(1)} %collective-permute-done.12.got_ref, bf16[2,1024,2048]{2,1,0:T(8,128)(2,1)S(1)} %left_focus.1.left_ref), custom_call_target="tpu_custom_call" | custom-call | flops 1073741824 | bytes 9175040 | tf_op jit(solution)/shard_map/product/pallas_call | solution.py:181
  22.7 3.7 %collective-permute-done.6.got_ref = bf16[4,2,16,1024]{3,2,1,0:T(8,128)(2,1)S(1)} collective-permute-done((bf16[4,2,16,1024]{3,2,1,0:T(8,128)(2,1)S(1)}, bf16[4,2,16,1024]{3,2,1,0:T(8,128)(2,1)S(1)}, u32[]{:S(2)}, u32[]{:S(2)}) %collective-permute-start.6) | collective-permute-done | bytes 262176 | tf_op jit(solution)/shard_map/ppermute | solution.py:333
  26.4 1.9 %product.5 = (f32[2,2,16,2048]{3,2,1,0:T(8,128)S(1)}, f32[2,2,16,2048]{3,2,1,0:T(8,128)S(1)}) custom-call(bf16[4,2,16,1024]{3,2,1,0:T(8,128)(2,1)S(1)} %get-tuple-element.44.own_ref, bf16[4,2,16,1024]{3,2,1,0:T(8,128)(2,1)S(1)} %collective-permute-done.6.got_ref, bf16[2,1024,2048]{2,1,0:T(8,128)(2,1)S(1)} %left_focus.1.left_ref), custom_call_target="tpu_custom_call" | custom-call | flops 1073741824 | bytes 9175040 | tf_op jit(solution)/shard_map/product/pallas_call | solution.py:181
  28.4 2.5 %collective-permute-done.got_ref = bf16[4,2,16,1024]{3,2,1,0:T(8,128)(2,1)S(1)} collective-permute-done((bf16[4,2,16,1024]{3,2,1,0:T(8,128)(2,1)S(1)}, bf16[4,2,16,1024]{3,2,1,0:T(8,128)(2,1)S(1)}, u32[]{:S(2)}, u32[]{:S(2)}) %collective-permute-start) | collective-permute-done | bytes 262176 | tf_op jit(solution)/shard_map/ppermute | solution.py:333
  30.9 1.9 %product.4 = (f32[2,2,16,2048]{3,2,1,0:T(8,128)S(1)}, f32[2,2,16,2048]{3,2,1,0:T(8,128)S(1)}) custom-call(bf16[4,2,16,1024]{3,2,1,0:T(8,128)(2,1)S(1)} %get-tuple-element.35.own_ref, bf16[4,2,16,1024]{3,2,1,0:T(8,128)(2,1)S(1)} %collective-permute-done.got_ref, bf16[2,1024,2048]{2,1,0:T(8,128)(2,1)S(1)} %left_focus.1.left_ref), custom_call_target="tpu_custom_call" | custom-call | flops 1073741824 | bytes 9175040 | tf_op jit(solution)/shard_map/product/pallas_call | solution.py:181
  32.9 2.5 %collective-permute-start.20 = (bf16[1,2,16,2048]{3,2,1,0:T(8,128)(2,1)S(1)}, bf16[1,2,16,2048]{3,2,1,0:T(8,128)(2,1)S(1)}, u32[]{:S(2)}, u32[]{:S(2)}) collective-permute-start(bf16[1,2,16,2048]{3,2,1,0:T(8,128)(2,1)S(1)} %get-tuple-element.62), channel_id=1, source_target_pairs={{0,2},{1,3},{2,0},{3,1},{4,6},{5,7},{6,4},{7,5},{8,10},{9,11},{10,... | collective-permute-start | bytes 393224 | tf_op jit(solution)/shard_map/ppermute | solution.py:199
  35.7 2.1 %collective-permute-start.8 = (bf16[1,2,16,2048]{3,2,1,0:T(8,128)(2,1)S(1)}, bf16[1,2,16,2048]{3,2,1,0:T(8,128)(2,1)S(1)}, u32[]{:S(2)}, u32[]{:S(2)}) collective-permute-start(bf16[1,2,16,2048]{3,2,1,0:T(8,128)(2,1)S(1)} %get-tuple-element.48), channel_id=1, source_target_pairs={{0,2},{1,3},{2,0},{3,1},{4,6},{5,7},{6,4},{7,5},{8,10},{9,11},{10,... | collective-permute-start | bytes 393224 | tf_op jit(solution)/shard_map/ppermute | solution.py:199
  37.9 1.9 %collective-permute-done.20.got_ref = bf16[1,2,16,2048]{3,2,1,0:T(8,128)(2,1)S(1)} collective-permute-done((bf16[1,2,16,2048]{3,2,1,0:T(8,128)(2,1)S(1)}, bf16[1,2,16,2048]{3,2,1,0:T(8,128)(2,1)S(1)}, u32[]{:S(2)}, u32[]{:S(2)}) %collective-permute-start.20) | collective-permute-done | bytes 131104 | tf_op jit(solution)/shard_map/ppermute | solution.py:199
  39.8 1.6 %collective-permute-start.21 = (bf16[16,2048]{1,0:T(8,128)(2,1)S(1)}, bf16[16,2048]{1,0:T(8,128)(2,1)S(1)}, u32[]{:S(2)}, u32[]{:S(2)}) collective-permute-start(bf16[16,2048]{1,0:T(8,128)(2,1)S(1)} %get-tuple-element.64), channel_id=1, source_target_pairs={{0,8},{8,0},{16,24},{24,16},{1,9},{9,1},{17,25},{25,17},{2,10},{10... | collective-permute-start | bytes 196616 | tf_op jit(solution)/shard_map/ppermute | solution.py:199
  42.6 1.6 %collective-permute-start.15 = (bf16[16,2048]{1,0:T(8,128)(2,1)S(1)}, bf16[16,2048]{1,0:T(8,128)(2,1)S(1)}, u32[]{:S(2)}, u32[]{:S(2)}) collective-permute-start(bf16[16,2048]{1,0:T(8,128)(2,1)S(1)} %get-tuple-element.57), channel_id=1, source_target_pairs={{0,8},{8,0},{16,24},{24,16},{1,9},{9,1},{17,25},{25,17},{2,10},{10... | collective-permute-start | bytes 196616 | tf_op jit(solution)/shard_map/ppermute | solution.py:199
  45.4 1.6 %collective-permute-start.9 = (bf16[16,2048]{1,0:T(8,128)(2,1)S(1)}, bf16[16,2048]{1,0:T(8,128)(2,1)S(1)}, u32[]{:S(2)}, u32[]{:S(2)}) collective-permute-start(bf16[16,2048]{1,0:T(8,128)(2,1)S(1)} %get-tuple-element.50), channel_id=1, source_target_pairs={{0,8},{8,0},{16,24},{24,16},{1,9},{9,1},{17,25},{25,17},{2,10},{10... | collective-permute-start | bytes 196616 | tf_op jit(solution)/shard_map/ppermute | solution.py:199
  48.1 1.6 %collective-permute-start.3 = (bf16[16,2048]{1,0:T(8,128)(2,1)S(1)}, bf16[16,2048]{1,0:T(8,128)(2,1)S(1)}, u32[]{:S(2)}, u32[]{:S(2)}) collective-permute-start(bf16[16,2048]{1,0:T(8,128)(2,1)S(1)} %get-tuple-element.43), channel_id=1, source_target_pairs={{0,8},{8,0},{16,24},{24,16},{1,9},{9,1},{17,25},{25,17},{2,10},{10... | collective-permute-start | bytes 196616 | tf_op jit(solution)/shard_map/ppermute | solution.py:199
  49.7 2.6 %collective-permute-start.22 = (bf16[16,2048]{1,0:T(8,128)(2,1)S(1)}, bf16[16,2048]{1,0:T(8,128)(2,1)S(1)}, u32[]{:S(2)}, u32[]{:S(2)}) collective-permute-start(bf16[16,2048]{1,0:T(8,128)(2,1)S(1)} %shard_map.51.a_ref), channel_id=1, source_target_pairs={{0,16},{8,24},{16,0},{24,8},{1,17},{9,25},{17,1},{25,9},{2,18},{10... | collective-permute-start | bytes 196616 | tf_op jit(solution)/shard_map/ppermute | solution.py:199
  52.8 2.6 %collective-permute-start.10 = (bf16[16,2048]{1,0:T(8,128)(2,1)S(1)}, bf16[16,2048]{1,0:T(8,128)(2,1)S(1)}, u32[]{:S(2)}, u32[]{:S(2)}) collective-permute-start(bf16[16,2048]{1,0:T(8,128)(2,1)S(1)} %shard_map.43.a_ref), channel_id=1, source_target_pairs={{0,16},{8,24},{16,0},{24,8},{1,17},{9,25},{17,1},{25,9},{2,18},{10... | collective-permute-start | bytes 196616 | tf_op jit(solution)/shard_map/ppermute | solution.py:199
  55.9 3.6 %collective-permute-done.22.b_ref = bf16[16,2048]{1,0:T(8,128)(2,1)S(1)} collective-permute-done((bf16[16,2048]{1,0:T(8,128)(2,1)S(1)}, bf16[16,2048]{1,0:T(8,128)(2,1)S(1)}, u32[]{:S(2)}, u32[]{:S(2)}) %collective-permute-start.22) | collective-permute-done | bytes 65568 | tf_op jit(solution)/shard_map/ppermute | solution.py:199
  65.5 1.4 %collective-permute-done.17.refs_3_ = bf16[16,2048]{1,0:T(8,128)(2,1)S(1)} collective-permute-done((bf16[16,2048]{1,0:T(8,128)(2,1)S(1)}, bf16[16,2048]{1,0:T(8,128)(2,1)S(1)}, u32[]{:S(2)}, u32[]{:S(2)}) %collective-permute-start.17) | collective-permute-done | bytes 65568 | tf_op jit(solution)/shard_map/ppermute | solution.py:199
  66.9 1.4 %collective-permute-done.11.refs_1_ = bf16[16,2048]{1,0:T(8,128)(2,1)S(1)} collective-permute-done((bf16[16,2048]{1,0:T(8,128)(2,1)S(1)}, bf16[16,2048]{1,0:T(8,128)(2,1)S(1)}, u32[]{:S(2)}, u32[]{:S(2)}) %collective-permute-start.11) | collective-permute-done | bytes 65568 | tf_op jit(solution)/shard_map/ppermute | solution.py:199
  (48 shorter events, 13.9 us)
Async XLA Ops:
  3.6 13.9 %collective-permute-start.18 = (bf16[4,2,16,1024]{3,2,1,0:T(8,128)(2,1)S(1)}, bf16[4,2,16,1024]{3,2,1,0:T(8,128)(2,1)S(1)}, u32[]{:S(2)}, u32[]{:S(2)}) collective-permute-start(bf16[4,2,16,1024]{3,2,1,0:T(8,128)(2,1)S(1)} %get-tuple-element.58.own_ref), channel_id=1, source_target_pairs={{0,4},{1,5},{6,2},{7,3},{8,12},{9,13},{14,10},{15,11},{16,20},{17,... | collective-permute-start | bytes 786440 | tf_op jit(solution)/shard_map/ppermute | solution.py:333
  8.5 12.3 %collective-permute-start.12 = (bf16[4,2,16,1024]{3,2,1,0:T(8,128)(2,1)S(1)}, bf16[4,2,16,1024]{3,2,1,0:T(8,128)(2,1)S(1)}, u32[]{:S(2)}, u32[]{:S(2)}) collective-permute-start(bf16[4,2,16,1024]{3,2,1,0:T(8,128)(2,1)S(1)} %get-tuple-element.51.own_ref), channel_id=1, source_target_pairs={{0,4},{1,5},{6,2},{7,3},{8,12},{9,13},{14,10},{15,11},{16,20},{17,... | collective-permute-start | bytes 786440 | tf_op jit(solution)/shard_map/ppermute | solution.py:333
  9.8 16.6 %collective-permute-start.6 = (bf16[4,2,16,1024]{3,2,1,0:T(8,128)(2,1)S(1)}, bf16[4,2,16,1024]{3,2,1,0:T(8,128)(2,1)S(1)}, u32[]{:S(2)}, u32[]{:S(2)}) collective-permute-start(bf16[4,2,16,1024]{3,2,1,0:T(8,128)(2,1)S(1)} %get-tuple-element.44.own_ref), channel_id=1, source_target_pairs={{0,4},{1,5},{6,2},{7,3},{8,12},{9,13},{14,10},{15,11},{16,20},{17,... | collective-permute-start | bytes 786440 | tf_op jit(solution)/shard_map/ppermute | solution.py:333
  11.1 19.8 %collective-permute-start = (bf16[4,2,16,1024]{3,2,1,0:T(8,128)(2,1)S(1)}, bf16[4,2,16,1024]{3,2,1,0:T(8,128)(2,1)S(1)}, u32[]{:S(2)}, u32[]{:S(2)}) collective-permute-start(bf16[4,2,16,1024]{3,2,1,0:T(8,128)(2,1)S(1)} %get-tuple-element.35.own_ref), channel_id=1, source_target_pairs={{0,4},{1,5},{6,2},{7,3},{8,12},{9,13},{14,10},{15,11},{16,20},{17,... | collective-permute-start | bytes 786440 | tf_op jit(solution)/shard_map/ppermute | solution.py:333
  19.4 13.5 %collective-permute-start.19 = (f32[2,2,16,2048]{3,2,1,0:T(8,128)S(1)}, f32[2,2,16,2048]{3,2,1,0:T(8,128)S(1)}, u32[]{:S(2)}, u32[]{:S(2)}) collective-permute-start(f32[2,2,16,2048]{3,2,1,0:T(8,128)S(1)} %get-tuple-element.60), channel_id=1, source_target_pairs={{0,1},{1,0},{2,3},{3,2},{4,5},{5,4},{6,7},{7,6},{8,9},{9,8},{10,11... | collective-permute-start | bytes 1572872 | tf_op jit(solution)/shard_map/ppermute | solution.py:199
  22.7 12.8 %collective-permute-start.13 = (f32[2,2,16,2048]{3,2,1,0:T(8,128)S(1)}, f32[2,2,16,2048]{3,2,1,0:T(8,128)S(1)}, u32[]{:S(2)}, u32[]{:S(2)}) collective-permute-start(f32[2,2,16,2048]{3,2,1,0:T(8,128)S(1)} %get-tuple-element.53), channel_id=1, source_target_pairs={{0,1},{1,0},{2,3},{3,2},{4,5},{5,4},{6,7},{7,6},{8,9},{9,8},{10,11... | collective-permute-start | bytes 1572872 | tf_op jit(solution)/shard_map/ppermute | solution.py:199
  28.3 7.3 %collective-permute-start.7 = (f32[2,2,16,2048]{3,2,1,0:T(8,128)S(1)}, f32[2,2,16,2048]{3,2,1,0:T(8,128)S(1)}, u32[]{:S(2)}, u32[]{:S(2)}) collective-permute-start(f32[2,2,16,2048]{3,2,1,0:T(8,128)S(1)} %get-tuple-element.46), channel_id=1, source_target_pairs={{0,1},{1,0},{2,3},{3,2},{4,5},{5,4},{6,7},{7,6},{8,9},{9,8},{10,11... | collective-permute-start | bytes 1572872 | tf_op jit(solution)/shard_map/ppermute | solution.py:199
  32.8 5.0 %collective-permute-start.1 = (f32[2,2,16,2048]{3,2,1,0:T(8,128)S(1)}, f32[2,2,16,2048]{3,2,1,0:T(8,128)S(1)}, u32[]{:S(2)}, u32[]{:S(2)}) collective-permute-start(f32[2,2,16,2048]{3,2,1,0:T(8,128)S(1)} %get-tuple-element.39), channel_id=1, source_target_pairs={{0,1},{1,0},{2,3},{3,2},{4,5},{5,4},{6,7},{7,6},{8,9},{9,8},{10,11... | collective-permute-start | bytes 1572872 | tf_op jit(solution)/shard_map/ppermute | solution.py:199
  32.9 6.9 %collective-permute-start.20 = (bf16[1,2,16,2048]{3,2,1,0:T(8,128)(2,1)S(1)}, bf16[1,2,16,2048]{3,2,1,0:T(8,128)(2,1)S(1)}, u32[]{:S(2)}, u32[]{:S(2)}) collective-permute-start(bf16[1,2,16,2048]{3,2,1,0:T(8,128)(2,1)S(1)} %get-tuple-element.62), channel_id=1, source_target_pairs={{0,2},{1,3},{2,0},{3,1},{4,6},{5,7},{6,4},{7,5},{8,10},{9,11},{10,... | collective-permute-start | bytes 393224 | tf_op jit(solution)/shard_map/ppermute | solution.py:199
  35.5 7.1 %collective-permute-start.14 = (bf16[1,2,16,2048]{3,2,1,0:T(8,128)(2,1)S(1)}, bf16[1,2,16,2048]{3,2,1,0:T(8,128)(2,1)S(1)}, u32[]{:S(2)}, u32[]{:S(2)}) collective-permute-start(bf16[1,2,16,2048]{3,2,1,0:T(8,128)(2,1)S(1)} %get-tuple-element.55), channel_id=1, source_target_pairs={{0,2},{1,3},{2,0},{3,1},{4,6},{5,7},{6,4},{7,5},{8,10},{9,11},{10,... | collective-permute-start | bytes 393224 | tf_op jit(solution)/shard_map/ppermute | solution.py:199
  35.7 9.8 %collective-permute-start.8 = (bf16[1,2,16,2048]{3,2,1,0:T(8,128)(2,1)S(1)}, bf16[1,2,16,2048]{3,2,1,0:T(8,128)(2,1)S(1)}, u32[]{:S(2)}, u32[]{:S(2)}) collective-permute-start(bf16[1,2,16,2048]{3,2,1,0:T(8,128)(2,1)S(1)} %get-tuple-element.48), channel_id=1, source_target_pairs={{0,2},{1,3},{2,0},{3,1},{4,6},{5,7},{6,4},{7,5},{8,10},{9,11},{10,... | collective-permute-start | bytes 393224 | tf_op jit(solution)/shard_map/ppermute | solution.py:199
  37.8 10.2 %collective-permute-start.2 = (bf16[1,2,16,2048]{3,2,1,0:T(8,128)(2,1)S(1)}, bf16[1,2,16,2048]{3,2,1,0:T(8,128)(2,1)S(1)}, u32[]{:S(2)}, u32[]{:S(2)}) collective-permute-start(bf16[1,2,16,2048]{3,2,1,0:T(8,128)(2,1)S(1)} %get-tuple-element.41), channel_id=1, source_target_pairs={{0,2},{1,3},{2,0},{3,1},{4,6},{5,7},{6,4},{7,5},{8,10},{9,11},{10,... | collective-permute-start | bytes 393224 | tf_op jit(solution)/shard_map/ppermute | solution.py:199
  39.8 9.9 %collective-permute-start.21 = (bf16[16,2048]{1,0:T(8,128)(2,1)S(1)}, bf16[16,2048]{1,0:T(8,128)(2,1)S(1)}, u32[]{:S(2)}, u32[]{:S(2)}) collective-permute-start(bf16[16,2048]{1,0:T(8,128)(2,1)S(1)} %get-tuple-element.64), channel_id=1, source_target_pairs={{0,8},{8,0},{16,24},{24,16},{1,9},{9,1},{17,25},{25,17},{2,10},{10... | collective-permute-start | bytes 196616 | tf_op jit(solution)/shard_map/ppermute | solution.py:199
  42.6 9.7 %collective-permute-start.15 = (bf16[16,2048]{1,0:T(8,128)(2,1)S(1)}, bf16[16,2048]{1,0:T(8,128)(2,1)S(1)}, u32[]{:S(2)}, u32[]{:S(2)}) collective-permute-start(bf16[16,2048]{1,0:T(8,128)(2,1)S(1)} %get-tuple-element.57), channel_id=1, source_target_pairs={{0,8},{8,0},{16,24},{24,16},{1,9},{9,1},{17,25},{25,17},{2,10},{10... | collective-permute-start | bytes 196616 | tf_op jit(solution)/shard_map/ppermute | solution.py:199
  45.4 7.3 %collective-permute-start.9 = (bf16[16,2048]{1,0:T(8,128)(2,1)S(1)}, bf16[16,2048]{1,0:T(8,128)(2,1)S(1)}, u32[]{:S(2)}, u32[]{:S(2)}) collective-permute-start(bf16[16,2048]{1,0:T(8,128)(2,1)S(1)} %get-tuple-element.50), channel_id=1, source_target_pairs={{0,8},{8,0},{16,24},{24,16},{1,9},{9,1},{17,25},{25,17},{2,10},{10... | collective-permute-start | bytes 196616 | tf_op jit(solution)/shard_map/ppermute | solution.py:199
  48.1 7.4 %collective-permute-start.3 = (bf16[16,2048]{1,0:T(8,128)(2,1)S(1)}, bf16[16,2048]{1,0:T(8,128)(2,1)S(1)}, u32[]{:S(2)}, u32[]{:S(2)}) collective-permute-start(bf16[16,2048]{1,0:T(8,128)(2,1)S(1)} %get-tuple-element.43), channel_id=1, source_target_pairs={{0,8},{8,0},{16,24},{24,16},{1,9},{9,1},{17,25},{25,17},{2,10},{10... | collective-permute-start | bytes 196616 | tf_op jit(solution)/shard_map/ppermute | solution.py:199
  49.7 9.8 %collective-permute-start.22 = (bf16[16,2048]{1,0:T(8,128)(2,1)S(1)}, bf16[16,2048]{1,0:T(8,128)(2,1)S(1)}, u32[]{:S(2)}, u32[]{:S(2)}) collective-permute-start(bf16[16,2048]{1,0:T(8,128)(2,1)S(1)} %shard_map.51.a_ref), channel_id=1, source_target_pairs={{0,16},{8,24},{16,0},{24,8},{1,17},{9,25},{17,1},{25,9},{2,18},{10... | collective-permute-start | bytes 196616 | tf_op jit(solution)/shard_map/ppermute | solution.py:199
  52.4 9.2 %collective-permute-start.16 = (bf16[16,2048]{1,0:T(8,128)(2,1)S(1)}, bf16[16,2048]{1,0:T(8,128)(2,1)S(1)}, u32[]{:S(2)}, u32[]{:S(2)}) collective-permute-start(bf16[16,2048]{1,0:T(8,128)(2,1)S(1)} %shard_map.47.a_ref), channel_id=1, source_target_pairs={{0,16},{8,24},{16,0},{24,8},{1,17},{9,25},{17,1},{25,9},{2,18},{10... | collective-permute-start | bytes 196616 | tf_op jit(solution)/shard_map/ppermute | solution.py:199
  52.8 10.2 %collective-permute-start.10 = (bf16[16,2048]{1,0:T(8,128)(2,1)S(1)}, bf16[16,2048]{1,0:T(8,128)(2,1)S(1)}, u32[]{:S(2)}, u32[]{:S(2)}) collective-permute-start(bf16[16,2048]{1,0:T(8,128)(2,1)S(1)} %shard_map.43.a_ref), channel_id=1, source_target_pairs={{0,16},{8,24},{16,0},{24,8},{1,17},{9,25},{17,1},{25,9},{2,18},{10... | collective-permute-start | bytes 196616 | tf_op jit(solution)/shard_map/ppermute | solution.py:199
  55.5 8.8 %collective-permute-start.4 = (bf16[16,2048]{1,0:T(8,128)(2,1)S(1)}, bf16[16,2048]{1,0:T(8,128)(2,1)S(1)}, u32[]{:S(2)}, u32[]{:S(2)}) collective-permute-start(bf16[16,2048]{1,0:T(8,128)(2,1)S(1)} %shard_map.39.a_ref), channel_id=1, source_target_pairs={{0,16},{8,24},{16,0},{24,8},{1,17},{9,25},{17,1},{25,9},{2,18},{10... | collective-permute-start | bytes 196616 | tf_op jit(solution)/shard_map/ppermute | solution.py:199
  59.5 6.0 %collective-permute-start.23 = (bf16[16,2048]{1,0:T(8,128)(2,1)S(1)}, bf16[16,2048]{1,0:T(8,128)(2,1)S(1)}, u32[]{:S(2)}, u32[]{:S(2)}) collective-permute-start(bf16[16,2048]{1,0:T(8,128)(2,1)S(1)} %shard_map.52.refs_4_), channel_id=1, source_target_pairs={{0,8},{8,0},{16,24},{24,16},{1,9},{9,1},{17,25},{25,17},{2,10},{10... | collective-permute-start | bytes 196616 | tf_op jit(solution)/shard_map/ppermute | solution.py:199
  61.6 5.3 %collective-permute-start.17 = (bf16[16,2048]{1,0:T(8,128)(2,1)S(1)}, bf16[16,2048]{1,0:T(8,128)(2,1)S(1)}, u32[]{:S(2)}, u32[]{:S(2)}) collective-permute-start(bf16[16,2048]{1,0:T(8,128)(2,1)S(1)} %shard_map.48.refs_2_), channel_id=1, source_target_pairs={{0,8},{8,0},{16,24},{24,16},{1,9},{9,1},{17,25},{25,17},{2,10},{10... | collective-permute-start | bytes 196616 | tf_op jit(solution)/shard_map/ppermute | solution.py:199
  63.0 5.3 %collective-permute-start.11 = (bf16[16,2048]{1,0:T(8,128)(2,1)S(1)}, bf16[16,2048]{1,0:T(8,128)(2,1)S(1)}, u32[]{:S(2)}, u32[]{:S(2)}) collective-permute-start(bf16[16,2048]{1,0:T(8,128)(2,1)S(1)} %shard_map.44.refs_0_), channel_id=1, source_target_pairs={{0,8},{8,0},{16,24},{24,16},{1,9},{9,1},{17,25},{25,17},{2,10},{10... | collective-permute-start | bytes 196616 | tf_op jit(solution)/shard_map/ppermute | solution.py:199
  64.3 5.0 %collective-permute-start.5 = (bf16[16,2048]{1,0:T(8,128)(2,1)S(1)}, bf16[16,2048]{1,0:T(8,128)(2,1)S(1)}, u32[]{:S(2)}, u32[]{:S(2)}) collective-permute-start(bf16[16,2048]{1,0:T(8,128)(2,1)S(1)} %shard_map.40.refs_0_), channel_id=1, source_target_pairs={{0,8},{8,0},{16,24},{24,16},{1,9},{9,1},{17,25},{25,17},{2,10},{10... | collective-permute-start | bytes 196616 | tf_op jit(solution)/shard_map/ppermute | solution.py:199

commit v2 on v1

--- a/solution.py
+++ b/solution.py
@@ -339,10 +339,11 @@
         for k in range(PARTS[i]):
             parts.append(reduce_chunk(len(parts), made[2 * k], made[2 * k + 1]))
     shape = (2, sum(pieces), tile_rows)
-    out, head = None, len(parts) - 1
+    out, head = None, len(parts) // 2
     if head:
         out = write(tuple(range(head)), 0, parts, shape, None)
-    return write((head,), shape[1] - parts[head][0].shape[-2], parts, shape, out)
+    first = sum(part[0].shape[-2] for part in parts[:head])
+    return write(tuple(range(head, len(parts))), first, parts, shape, out)
 
 
 def solution(mesh):

time: 70.2 us -> 70.1 us (level)
  transfers between devices with their start and end apart: 24 -> 24, of which waited for: 14 -> 15; matrix products, arithmetic and copies ran while one was open for 0% -> 0% of each run, Pallas kernels for 20% -> 20%
where the time goes in v2:
time: 70.1 us; the launch traced here: 69.9 us
  starting transfers between devices  29.9 us (43%)
  waiting for transfers between devices  21.5 us (31%)
  Pallas kernels  18.2 us (26%)
    ppermute x20, starting transfers between devices, swap(): return lax.ppermute(value, axis, [(i, i ^ bit) for i in range(count)])  21.1 us
    ppermute x20, waiting for transfers between devices, swap(): return lax.ppermute(value, axis, [(i, i ^ bit) for i in range(count)])  14 us
    ppermute x4, starting transfers between devices, local(): got.append(lax.ppermute(own[i], ('row', 'col'), pairs))  8.83 us
    pallas_call x4, Pallas kernels, product(): pl.pallas_call(functools.partial(product_kernel, own_row, parts), in_spec...  7.53 us
    ppermute x4, waiting for transfers between devices, local(): got.append(lax.ppermute(own[i], ('row', 'col'), pairs))  7.49 us
    pallas_call x1, Pallas kernels, left_focus(): pl.pallas_call(left_kernel, in_specs=[VMEM, VMEM, HBM], out_specs=VMEM, o...  5.02 us
    pallas_call x1, Pallas kernels, weights(): pl.pallas_call(functools.partial(weights_kernel, pieces, count, per_row,...  3.57 us
    pallas_call x2, Pallas kernels, write(): pl.pallas_call(functools.partial(write_kernel, chunks, first), in_specs=[...  1.69 us
  transfers between devices with their start and end apart: 24, of which 15 were waited for; matrix products, arithmetic and copies ran while one was open for 0% of the time, Pallas kernels for 20%

profile of v2, /device:TPU:0, one launch (start us, length us, event | category | flops | bytes accessed | tf_op | source)
XLA Modules:
  0.0 69.9 jit_solution(4590619449649570308)
XLA Ops:
  0.0 3.6 %weights.1 = (bf16[4,2,16,1024]{3,2,1,0:T(8,128)(2,1)S(1)}, bf16[4,2,16,1024]{3,2,1,0:T(8,128)(2,1)S(1)}, bf16[4,2,16,1024]{3,2,1,0:T(8,128)(2,1)S(1)}, bf16[4,2...) custom-call(bf16[2,8,256,256]{3,2,1,0:T(8,128)(2,1)} %bitcast.4, ...), custom_call_target="tpu_custom_call" | custom-call | flops 536870912 | bytes 3145728 | tf_op jit(solution)/shard_map/weights/pallas_call | solution.py:129
  3.6 4.9 %collective-permute-start.18 = (bf16[4,2,16,1024]{3,2,1,0:T(8,128)(2,1)S(1)}, bf16[4,2,16,1024]{3,2,1,0:T(8,128)(2,1)S(1)}, u32[]{:S(2)}, u32[]{:S(2)}) collective-permute-start(bf16[4,2,16,1024]{3,2,1,0:T(8,128)(2,1)S(1)} %get-tuple-element.58.own_ref), channel_id=1, source_target_pairs={{0,4},{1,5},{6,2},{7,3},{8,12},{9,13},{14,10},{15,11},{16,20},{17,... | collective-permute-start | bytes 786440 | tf_op jit(solution)/shard_map/ppermute | solution.py:333
  8.5 1.3 %collective-permute-start.12 = (bf16[4,2,16,1024]{3,2,1,0:T(8,128)(2,1)S(1)}, bf16[4,2,16,1024]{3,2,1,0:T(8,128)(2,1)S(1)}, u32[]{:S(2)}, u32[]{:S(2)}) collective-permute-start(bf16[4,2,16,1024]{3,2,1,0:T(8,128)(2,1)S(1)} %get-tuple-element.51.own_ref), channel_id=1, source_target_pairs={{0,4},{1,5},{6,2},{7,3},{8,12},{9,13},{14,10},{15,11},{16,20},{17,... | collective-permute-start | bytes 786440 | tf_op jit(solution)/shard_map/ppermute | solution.py:333
  9.8 1.3 %collective-permute-start.6 = (bf16[4,2,16,1024]{3,2,1,0:T(8,128)(2,1)S(1)}, bf16[4,2,16,1024]{3,2,1,0:T(8,128)(2,1)S(1)}, u32[]{:S(2)}, u32[]{:S(2)}) collective-permute-start(bf16[4,2,16,1024]{3,2,1,0:T(8,128)(2,1)S(1)} %get-tuple-element.44.own_ref), channel_id=1, source_target_pairs={{0,4},{1,5},{6,2},{7,3},{8,12},{9,13},{14,10},{15,11},{16,20},{17,... | collective-permute-start | bytes 786440 | tf_op jit(solution)/shard_map/ppermute | solution.py:333
  11.1 1.3 %collective-permute-start = (bf16[4,2,16,1024]{3,2,1,0:T(8,128)(2,1)S(1)}, bf16[4,2,16,1024]{3,2,1,0:T(8,128)(2,1)S(1)}, u32[]{:S(2)}, u32[]{:S(2)}) collective-permute-start(bf16[4,2,16,1024]{3,2,1,0:T(8,128)(2,1)S(1)} %get-tuple-element.35.own_ref), channel_id=1, source_target_pairs={{0,4},{1,5},{6,2},{7,3},{8,12},{9,13},{14,10},{15,11},{16,20},{17,... | collective-permute-start | bytes 786440 | tf_op jit(solution)/shard_map/ppermute | solution.py:333
  12.4 5.0 %left_focus.1.left_ref = bf16[2,1024,2048]{2,1,0:T(8,128)(2,1)S(1)} custom-call(bf16[2,8,256,256]{3,2,1,0:T(8,128)(2,1)S(1)} %get-tuple-element.36.g_ref, bf16[2,1024,1024]{2,1,0:T(8,128)(2,1)S(1)} %get-tuple-element.37.first_ref, bf16[2,2048,1024]{2,1,0:T(8,128)(2,1)} %bitcast.3), custom_call_target="tpu_custom_call" | custom-call | flops 4294967296 | bytes 18874368 | tf_op jit(solution)/shard_map/left_focus/pallas_call | solution.py:59
  17.5 1.9 %product.7 = (f32[2,2,16,2048]{3,2,1,0:T(8,128)S(1)}, f32[2,2,16,2048]{3,2,1,0:T(8,128)S(1)}) custom-call(bf16[4,2,16,1024]{3,2,1,0:T(8,128)(2,1)S(1)} %get-tuple-element.58.own_ref, bf16[4,2,16,1024]{3,2,1,0:T(8,128)(2,1)S(1)} %collective-permute-done.18.got_ref, bf16[2,1024,2048]{2,1,0:T(8,128)(2,1)S(1)} %left_focus.1.left_ref), custom_call_target="tpu_custom_call" | custom-call | flops 1073741824 | bytes 9175040 | tf_op jit(solution)/shard_map/product/pallas_call | solution.py:181
  19.5 1.3 %collective-permute-done.12.got_ref = bf16[4,2,16,1024]{3,2,1,0:T(8,128)(2,1)S(1)} collective-permute-done((bf16[4,2,16,1024]{3,2,1,0:T(8,128)(2,1)S(1)}, bf16[4,2,16,1024]{3,2,1,0:T(8,128)(2,1)S(1)}, u32[]{:S(2)}, u32[]{:S(2)}) %collective-permute-start.12) | collective-permute-done | bytes 262176 | tf_op jit(solution)/shard_map/ppermute | solution.py:333
  20.8 1.9 %product.6 = (f32[2,2,16,2048]{3,2,1,0:T(8,128)S(1)}, f32[2,2,16,2048]{3,2,1,0:T(8,128)S(1)}) custom-call(bf16[4,2,16,1024]{3,2,1,0:T(8,128)(2,1)S(1)} %get-tuple-element.51.own_ref, bf16[4,2,16,1024]{3,2,1,0:T(8,128)(2,1)S(1)} %collective-permute-done.12.got_ref, bf16[2,1024,2048]{2,1,0:T(8,128)(2,1)S(1)} %left_focus.1.left_ref), custom_call_target="tpu_custom_call" | custom-call | flops 1073741824 | bytes 9175040 | tf_op jit(solution)/shard_map/product/pallas_call | solution.py:181
  22.7 3.7 %collective-permute-done.6.got_ref = bf16[4,2,16,1024]{3,2,1,0:T(8,128)(2,1)S(1)} collective-permute-done((bf16[4,2,16,1024]{3,2,1,0:T(8,128)(2,1)S(1)}, bf16[4,2,16,1024]{3,2,1,0:T(8,128)(2,1)S(1)}, u32[]{:S(2)}, u32[]{:S(2)}) %collective-permute-start.6) | collective-permute-done | bytes 262176 | tf_op jit(solution)/shard_map/ppermute | solution.py:333
  26.4 1.9 %product.5 = (f32[2,2,16,2048]{3,2,1,0:T(8,128)S(1)}, f32[2,2,16,2048]{3,2,1,0:T(8,128)S(1)}) custom-call(bf16[4,2,16,1024]{3,2,1,0:T(8,128)(2,1)S(1)} %get-tuple-element.44.own_ref, bf16[4,2,16,1024]{3,2,1,0:T(8,128)(2,1)S(1)} %collective-permute-done.6.got_ref, bf16[2,1024,2048]{2,1,0:T(8,128)(2,1)S(1)} %left_focus.1.left_ref), custom_call_target="tpu_custom_call" | custom-call | flops 1073741824 | bytes 9175040 | tf_op jit(solution)/shard_map/product/pallas_call | solution.py:181
  28.4 2.5 %collective-permute-done.got_ref = bf16[4,2,16,1024]{3,2,1,0:T(8,128)(2,1)S(1)} collective-permute-done((bf16[4,2,16,1024]{3,2,1,0:T(8,128)(2,1)S(1)}, bf16[4,2,16,1024]{3,2,1,0:T(8,128)(2,1)S(1)}, u32[]{:S(2)}, u32[]{:S(2)}) %collective-permute-start) | collective-permute-done | bytes 262176 | tf_op jit(solution)/shard_map/ppermute | solution.py:333
  30.9 1.9 %product.4 = (f32[2,2,16,2048]{3,2,1,0:T(8,128)S(1)}, f32[2,2,16,2048]{3,2,1,0:T(8,128)S(1)}) custom-call(bf16[4,2,16,1024]{3,2,1,0:T(8,128)(2,1)S(1)} %get-tuple-element.35.own_ref, bf16[4,2,16,1024]{3,2,1,0:T(8,128)(2,1)S(1)} %collective-permute-done.got_ref, bf16[2,1024,2048]{2,1,0:T(8,128)(2,1)S(1)} %left_focus.1.left_ref), custom_call_target="tpu_custom_call" | custom-call | flops 1073741824 | bytes 9175040 | tf_op jit(solution)/shard_map/product/pallas_call | solution.py:181
  32.9 2.5 %collective-permute-start.20 = (bf16[1,2,16,2048]{3,2,1,0:T(8,128)(2,1)S(1)}, bf16[1,2,16,2048]{3,2,1,0:T(8,128)(2,1)S(1)}, u32[]{:S(2)}, u32[]{:S(2)}) collective-permute-start(bf16[1,2,16,2048]{3,2,1,0:T(8,128)(2,1)S(1)} %get-tuple-element.62), channel_id=1, source_target_pairs={{0,2},{1,3},{2,0},{3,1},{4,6},{5,7},{6,4},{7,5},{8,10},{9,11},{10,... | collective-permute-start | bytes 393224 | tf_op jit(solution)/shard_map/ppermute | solution.py:199
  35.7 2.1 %collective-permute-start.8 = (bf16[1,2,16,2048]{3,2,1,0:T(8,128)(2,1)S(1)}, bf16[1,2,16,2048]{3,2,1,0:T(8,128)(2,1)S(1)}, u32[]{:S(2)}, u32[]{:S(2)}) collective-permute-start(bf16[1,2,16,2048]{3,2,1,0:T(8,128)(2,1)S(1)} %get-tuple-element.48), channel_id=1, source_target_pairs={{0,2},{1,3},{2,0},{3,1},{4,6},{5,7},{6,4},{7,5},{8,10},{9,11},{10,... | collective-permute-start | bytes 393224 | tf_op jit(solution)/shard_map/ppermute | solution.py:199
  37.9 1.9 %collective-permute-done.20.got_ref = bf16[1,2,16,2048]{3,2,1,0:T(8,128)(2,1)S(1)} collective-permute-done((bf16[1,2,16,2048]{3,2,1,0:T(8,128)(2,1)S(1)}, bf16[1,2,16,2048]{3,2,1,0:T(8,128)(2,1)S(1)}, u32[]{:S(2)}, u32[]{:S(2)}) %collective-permute-start.20) | collective-permute-done | bytes 131104 | tf_op jit(solution)/shard_map/ppermute | solution.py:199
  39.8 1.6 %collective-permute-start.21 = (bf16[16,2048]{1,0:T(8,128)(2,1)S(1)}, bf16[16,2048]{1,0:T(8,128)(2,1)S(1)}, u32[]{:S(2)}, u32[]{:S(2)}) collective-permute-start(bf16[16,2048]{1,0:T(8,128)(2,1)S(1)} %get-tuple-element.64), channel_id=1, source_target_pairs={{0,8},{8,0},{16,24},{24,16},{1,9},{9,1},{17,25},{25,17},{2,10},{10... | collective-permute-start | bytes 196616 | tf_op jit(solution)/shard_map/ppermute | solution.py:199
  42.6 1.6 %collective-permute-start.15 = (bf16[16,2048]{1,0:T(8,128)(2,1)S(1)}, bf16[16,2048]{1,0:T(8,128)(2,1)S(1)}, u32[]{:S(2)}, u32[]{:S(2)}) collective-permute-start(bf16[16,2048]{1,0:T(8,128)(2,1)S(1)} %get-tuple-element.57), channel_id=1, source_target_pairs={{0,8},{8,0},{16,24},{24,16},{1,9},{9,1},{17,25},{25,17},{2,10},{10... | collective-permute-start | bytes 196616 | tf_op jit(solution)/shard_map/ppermute | solution.py:199
  45.4 1.6 %collective-permute-start.9 = (bf16[16,2048]{1,0:T(8,128)(2,1)S(1)}, bf16[16,2048]{1,0:T(8,128)(2,1)S(1)}, u32[]{:S(2)}, u32[]{:S(2)}) collective-permute-start(bf16[16,2048]{1,0:T(8,128)(2,1)S(1)} %get-tuple-element.50), channel_id=1, source_target_pairs={{0,8},{8,0},{16,24},{24,16},{1,9},{9,1},{17,25},{25,17},{2,10},{10... | collective-permute-start | bytes 196616 | tf_op jit(solution)/shard_map/ppermute | solution.py:199
  48.1 1.6 %collective-permute-start.3 = (bf16[16,2048]{1,0:T(8,128)(2,1)S(1)}, bf16[16,2048]{1,0:T(8,128)(2,1)S(1)}, u32[]{:S(2)}, u32[]{:S(2)}) collective-permute-start(bf16[16,2048]{1,0:T(8,128)(2,1)S(1)} %get-tuple-element.43), channel_id=1, source_target_pairs={{0,8},{8,0},{16,24},{24,16},{1,9},{9,1},{17,25},{25,17},{2,10},{10... | collective-permute-start | bytes 196616 | tf_op jit(solution)/shard_map/ppermute | solution.py:199
  49.7 2.6 %collective-permute-start.22 = (bf16[16,2048]{1,0:T(8,128)(2,1)S(1)}, bf16[16,2048]{1,0:T(8,128)(2,1)S(1)}, u32[]{:S(2)}, u32[]{:S(2)}) collective-permute-start(bf16[16,2048]{1,0:T(8,128)(2,1)S(1)} %shard_map.51.a_ref), channel_id=1, source_target_pairs={{0,16},{8,24},{16,0},{24,8},{1,17},{9,25},{17,1},{25,9},{2,18},{10... | collective-permute-start | bytes 196616 | tf_op jit(solution)/shard_map/ppermute | solution.py:199
  52.8 2.6 %collective-permute-start.10 = (bf16[16,2048]{1,0:T(8,128)(2,1)S(1)}, bf16[16,2048]{1,0:T(8,128)(2,1)S(1)}, u32[]{:S(2)}, u32[]{:S(2)}) collective-permute-start(bf16[16,2048]{1,0:T(8,128)(2,1)S(1)} %shard_map.43.a_ref), channel_id=1, source_target_pairs={{0,16},{8,24},{16,0},{24,8},{1,17},{9,25},{17,1},{25,9},{2,18},{10... | collective-permute-start | bytes 196616 | tf_op jit(solution)/shard_map/ppermute | solution.py:199
  55.9 3.6 %collective-permute-done.22.b_ref = bf16[16,2048]{1,0:T(8,128)(2,1)S(1)} collective-permute-done((bf16[16,2048]{1,0:T(8,128)(2,1)S(1)}, bf16[16,2048]{1,0:T(8,128)(2,1)S(1)}, u32[]{:S(2)}, u32[]{:S(2)}) %collective-permute-start.22) | collective-permute-done | bytes 65568 | tf_op jit(solution)/shard_map/ppermute | solution.py:199
  65.5 1.4 %collective-permute-done.17.refs_1_ = bf16[16,2048]{1,0:T(8,128)(2,1)S(1)} collective-permute-done((bf16[16,2048]{1,0:T(8,128)(2,1)S(1)}, bf16[16,2048]{1,0:T(8,128)(2,1)S(1)}, u32[]{:S(2)}, u32[]{:S(2)}) %collective-permute-start.17) | collective-permute-done | bytes 65568 | tf_op jit(solution)/shard_map/ppermute | solution.py:199
  (48 shorter events, 13.9 us)
Async XLA Ops:
  3.6 13.9 %collective-permute-start.18 = (bf16[4,2,16,1024]{3,2,1,0:T(8,128)(2,1)S(1)}, bf16[4,2,16,1024]{3,2,1,0:T(8,128)(2,1)S(1)}, u32[]{:S(2)}, u32[]{:S(2)}) collective-permute-start(bf16[4,2,16,1024]{3,2,1,0:T(8,128)(2,1)S(1)} %get-tuple-element.58.own_ref), channel_id=1, source_target_pairs={{0,4},{1,5},{6,2},{7,3},{8,12},{9,13},{14,10},{15,11},{16,20},{17,... | collective-permute-start | bytes 786440 | tf_op jit(solution)/shard_map/ppermute | solution.py:333
  8.5 12.3 %collective-permute-start.12 = (bf16[4,2,16,1024]{3,2,1,0:T(8,128)(2,1)S(1)}, bf16[4,2,16,1024]{3,2,1,0:T(8,128)(2,1)S(1)}, u32[]{:S(2)}, u32[]{:S(2)}) collective-permute-start(bf16[4,2,16,1024]{3,2,1,0:T(8,128)(2,1)S(1)} %get-tuple-element.51.own_ref), channel_id=1, source_target_pairs={{0,4},{1,5},{6,2},{7,3},{8,12},{9,13},{14,10},{15,11},{16,20},{17,... | collective-permute-start | bytes 786440 | tf_op jit(solution)/shard_map/ppermute | solution.py:333
  9.8 16.6 %collective-permute-start.6 = (bf16[4,2,16,1024]{3,2,1,0:T(8,128)(2,1)S(1)}, bf16[4,2,16,1024]{3,2,1,0:T(8,128)(2,1)S(1)}, u32[]{:S(2)}, u32[]{:S(2)}) collective-permute-start(bf16[4,2,16,1024]{3,2,1,0:T(8,128)(2,1)S(1)} %get-tuple-element.44.own_ref), channel_id=1, source_target_pairs={{0,4},{1,5},{6,2},{7,3},{8,12},{9,13},{14,10},{15,11},{16,20},{17,... | collective-permute-start | bytes 786440 | tf_op jit(solution)/shard_map/ppermute | solution.py:333
  11.1 19.8 %collective-permute-start = (bf16[4,2,16,1024]{3,2,1,0:T(8,128)(2,1)S(1)}, bf16[4,2,16,1024]{3,2,1,0:T(8,128)(2,1)S(1)}, u32[]{:S(2)}, u32[]{:S(2)}) collective-permute-start(bf16[4,2,16,1024]{3,2,1,0:T(8,128)(2,1)S(1)} %get-tuple-element.35.own_ref), channel_id=1, source_target_pairs={{0,4},{1,5},{6,2},{7,3},{8,12},{9,13},{14,10},{15,11},{16,20},{17,... | collective-permute-start | bytes 786440 | tf_op jit(solution)/shard_map/ppermute | solution.py:333
  19.4 13.5 %collective-permute-start.19 = (f32[2,2,16,2048]{3,2,1,0:T(8,128)S(1)}, f32[2,2,16,2048]{3,2,1,0:T(8,128)S(1)}, u32[]{:S(2)}, u32[]{:S(2)}) collective-permute-start(f32[2,2,16,2048]{3,2,1,0:T(8,128)S(1)} %get-tuple-element.60), channel_id=1, source_target_pairs={{0,1},{1,0},{2,3},{3,2},{4,5},{5,4},{6,7},{7,6},{8,9},{9,8},{10,11... | collective-permute-start | bytes 1572872 | tf_op jit(solution)/shard_map/ppermute | solution.py:199
  22.7 12.8 %collective-permute-start.13 = (f32[2,2,16,2048]{3,2,1,0:T(8,128)S(1)}, f32[2,2,16,2048]{3,2,1,0:T(8,128)S(1)}, u32[]{:S(2)}, u32[]{:S(2)}) collective-permute-start(f32[2,2,16,2048]{3,2,1,0:T(8,128)S(1)} %get-tuple-element.53), channel_id=1, source_target_pairs={{0,1},{1,0},{2,3},{3,2},{4,5},{5,4},{6,7},{7,6},{8,9},{9,8},{10,11... | collective-permute-start | bytes 1572872 | tf_op jit(solution)/shard_map/ppermute | solution.py:199
  28.3 7.3 %collective-permute-start.7 = (f32[2,2,16,2048]{3,2,1,0:T(8,128)S(1)}, f32[2,2,16,2048]{3,2,1,0:T(8,128)S(1)}, u32[]{:S(2)}, u32[]{:S(2)}) collective-permute-start(f32[2,2,16,2048]{3,2,1,0:T(8,128)S(1)} %get-tuple-element.46), channel_id=1, source_target_pairs={{0,1},{1,0},{2,3},{3,2},{4,5},{5,4},{6,7},{7,6},{8,9},{9,8},{10,11... | collective-permute-start | bytes 1572872 | tf_op jit(solution)/shard_map/ppermute | solution.py:199
  32.8 5.0 %collective-permute-start.1 = (f32[2,2,16,2048]{3,2,1,0:T(8,128)S(1)}, f32[2,2,16,2048]{3,2,1,0:T(8,128)S(1)}, u32[]{:S(2)}, u32[]{:S(2)}) collective-permute-start(f32[2,2,16,2048]{3,2,1,0:T(8,128)S(1)} %get-tuple-element.39), channel_id=1, source_target_pairs={{0,1},{1,0},{2,3},{3,2},{4,5},{5,4},{6,7},{7,6},{8,9},{9,8},{10,11... | collective-permute-start | bytes 1572872 | tf_op jit(solution)/shard_map/ppermute | solution.py:199
  32.9 6.9 %collective-permute-start.20 = (bf16[1,2,16,2048]{3,2,1,0:T(8,128)(2,1)S(1)}, bf16[1,2,16,2048]{3,2,1,0:T(8,128)(2,1)S(1)}, u32[]{:S(2)}, u32[]{:S(2)}) collective-permute-start(bf16[1,2,16,2048]{3,2,1,0:T(8,128)(2,1)S(1)} %get-tuple-element.62), channel_id=1, source_target_pairs={{0,2},{1,3},{2,0},{3,1},{4,6},{5,7},{6,4},{7,5},{8,10},{9,11},{10,... | collective-permute-start | bytes 393224 | tf_op jit(solution)/shard_map/ppermute | solution.py:199
  35.5 7.1 %collective-permute-start.14 = (bf16[1,2,16,2048]{3,2,1,0:T(8,128)(2,1)S(1)}, bf16[1,2,16,2048]{3,2,1,0:T(8,128)(2,1)S(1)}, u32[]{:S(2)}, u32[]{:S(2)}) collective-permute-start(bf16[1,2,16,2048]{3,2,1,0:T(8,128)(2,1)S(1)} %get-tuple-element.55), channel_id=1, source_target_pairs={{0,2},{1,3},{2,0},{3,1},{4,6},{5,7},{6,4},{7,5},{8,10},{9,11},{10,... | collective-permute-start | bytes 393224 | tf_op jit(solution)/shard_map/ppermute | solution.py:199
  35.7 9.8 %collective-permute-start.8 = (bf16[1,2,16,2048]{3,2,1,0:T(8,128)(2,1)S(1)}, bf16[1,2,16,2048]{3,2,1,0:T(8,128)(2,1)S(1)}, u32[]{:S(2)}, u32[]{:S(2)}) collective-permute-start(bf16[1,2,16,2048]{3,2,1,0:T(8,128)(2,1)S(1)} %get-tuple-element.48), channel_id=1, source_target_pairs={{0,2},{1,3},{2,0},{3,1},{4,6},{5,7},{6,4},{7,5},{8,10},{9,11},{10,... | collective-permute-start | bytes 393224 | tf_op jit(solution)/shard_map/ppermute | solution.py:199
  37.8 10.2 %collective-permute-start.2 = (bf16[1,2,16,2048]{3,2,1,0:T(8,128)(2,1)S(1)}, bf16[1,2,16,2048]{3,2,1,0:T(8,128)(2,1)S(1)}, u32[]{:S(2)}, u32[]{:S(2)}) collective-permute-start(bf16[1,2,16,2048]{3,2,1,0:T(8,128)(2,1)S(1)} %get-tuple-element.41), channel_id=1, source_target_pairs={{0,2},{1,3},{2,0},{3,1},{4,6},{5,7},{6,4},{7,5},{8,10},{9,11},{10,... | collective-permute-start | bytes 393224 | tf_op jit(solution)/shard_map/ppermute | solution.py:199
  39.8 9.9 %collective-permute-start.21 = (bf16[16,2048]{1,0:T(8,128)(2,1)S(1)}, bf16[16,2048]{1,0:T(8,128)(2,1)S(1)}, u32[]{:S(2)}, u32[]{:S(2)}) collective-permute-start(bf16[16,2048]{1,0:T(8,128)(2,1)S(1)} %get-tuple-element.64), channel_id=1, source_target_pairs={{0,8},{8,0},{16,24},{24,16},{1,9},{9,1},{17,25},{25,17},{2,10},{10... | collective-permute-start | bytes 196616 | tf_op jit(solution)/shard_map/ppermute | solution.py:199
  42.6 9.7 %collective-permute-start.15 = (bf16[16,2048]{1,0:T(8,128)(2,1)S(1)}, bf16[16,2048]{1,0:T(8,128)(2,1)S(1)}, u32[]{:S(2)}, u32[]{:S(2)}) collective-permute-start(bf16[16,2048]{1,0:T(8,128)(2,1)S(1)} %get-tuple-element.57), channel_id=1, source_target_pairs={{0,8},{8,0},{16,24},{24,16},{1,9},{9,1},{17,25},{25,17},{2,10},{10... | collective-permute-start | bytes 196616 | tf_op jit(solution)/shard_map/ppermute | solution.py:199
  45.4 7.3 %collective-permute-start.9 = (bf16[16,2048]{1,0:T(8,128)(2,1)S(1)}, bf16[16,2048]{1,0:T(8,128)(2,1)S(1)}, u32[]{:S(2)}, u32[]{:S(2)}) collective-permute-start(bf16[16,2048]{1,0:T(8,128)(2,1)S(1)} %get-tuple-element.50), channel_id=1, source_target_pairs={{0,8},{8,0},{16,24},{24,16},{1,9},{9,1},{17,25},{25,17},{2,10},{10... | collective-permute-start | bytes 196616 | tf_op jit(solution)/shard_map/ppermute | solution.py:199
  48.1 7.4 %collective-permute-start.3 = (bf16[16,2048]{1,0:T(8,128)(2,1)S(1)}, bf16[16,2048]{1,0:T(8,128)(2,1)S(1)}, u32[]{:S(2)}, u32[]{:S(2)}) collective-permute-start(bf16[16,2048]{1,0:T(8,128)(2,1)S(1)} %get-tuple-element.43), channel_id=1, source_target_pairs={{0,8},{8,0},{16,24},{24,16},{1,9},{9,1},{17,25},{25,17},{2,10},{10... | collective-permute-start | bytes 196616 | tf_op jit(solution)/shard_map/ppermute | solution.py:199
  49.7 9.8 %collective-permute-start.22 = (bf16[16,2048]{1,0:T(8,128)(2,1)S(1)}, bf16[16,2048]{1,0:T(8,128)(2,1)S(1)}, u32[]{:S(2)}, u32[]{:S(2)}) collective-permute-start(bf16[16,2048]{1,0:T(8,128)(2,1)S(1)} %shard_map.51.a_ref), channel_id=1, source_target_pairs={{0,16},{8,24},{16,0},{24,8},{1,17},{9,25},{17,1},{25,9},{2,18},{10... | collective-permute-start | bytes 196616 | tf_op jit(solution)/shard_map/ppermute | solution.py:199
  52.4 9.2 %collective-permute-start.16 = (bf16[16,2048]{1,0:T(8,128)(2,1)S(1)}, bf16[16,2048]{1,0:T(8,128)(2,1)S(1)}, u32[]{:S(2)}, u32[]{:S(2)}) collective-permute-start(bf16[16,2048]{1,0:T(8,128)(2,1)S(1)} %shard_map.47.a_ref), channel_id=1, source_target_pairs={{0,16},{8,24},{16,0},{24,8},{1,17},{9,25},{17,1},{25,9},{2,18},{10... | collective-permute-start | bytes 196616 | tf_op jit(solution)/shard_map/ppermute | solution.py:199
  52.8 10.2 %collective-permute-start.10 = (bf16[16,2048]{1,0:T(8,128)(2,1)S(1)}, bf16[16,2048]{1,0:T(8,128)(2,1)S(1)}, u32[]{:S(2)}, u32[]{:S(2)}) collective-permute-start(bf16[16,2048]{1,0:T(8,128)(2,1)S(1)} %shard_map.43.a_ref), channel_id=1, source_target_pairs={{0,16},{8,24},{16,0},{24,8},{1,17},{9,25},{17,1},{25,9},{2,18},{10... | collective-permute-start | bytes 196616 | tf_op jit(solution)/shard_map/ppermute | solution.py:199
  55.5 8.8 %collective-permute-start.4 = (bf16[16,2048]{1,0:T(8,128)(2,1)S(1)}, bf16[16,2048]{1,0:T(8,128)(2,1)S(1)}, u32[]{:S(2)}, u32[]{:S(2)}) collective-permute-start(bf16[16,2048]{1,0:T(8,128)(2,1)S(1)} %shard_map.39.a_ref), channel_id=1, source_target_pairs={{0,16},{8,24},{16,0},{24,8},{1,17},{9,25},{17,1},{25,9},{2,18},{10... | collective-permute-start | bytes 196616 | tf_op jit(solution)/shard_map/ppermute | solution.py:199
  59.5 6.0 %collective-permute-start.23 = (bf16[16,2048]{1,0:T(8,128)(2,1)S(1)}, bf16[16,2048]{1,0:T(8,128)(2,1)S(1)}, u32[]{:S(2)}, u32[]{:S(2)}) collective-permute-start(bf16[16,2048]{1,0:T(8,128)(2,1)S(1)} %shard_map.52.refs_2_), channel_id=1, source_target_pairs={{0,8},{8,0},{16,24},{24,16},{1,9},{9,1},{17,25},{25,17},{2,10},{10... | collective-permute-start | bytes 196616 | tf_op jit(solution)/shard_map/ppermute | solution.py:199
  61.6 5.3 %collective-permute-start.17 = (bf16[16,2048]{1,0:T(8,128)(2,1)S(1)}, bf16[16,2048]{1,0:T(8,128)(2,1)S(1)}, u32[]{:S(2)}, u32[]{:S(2)}) collective-permute-start(bf16[16,2048]{1,0:T(8,128)(2,1)S(1)} %shard_map.48.refs_0_), channel_id=1, source_target_pairs={{0,8},{8,0},{16,24},{24,16},{1,9},{9,1},{17,25},{25,17},{2,10},{10... | collective-permute-start | bytes 196616 | tf_op jit(solution)/shard_map/ppermute | solution.py:199
  63.0 5.3 %collective-permute-start.11 = (bf16[16,2048]{1,0:T(8,128)(2,1)S(1)}, bf16[16,2048]{1,0:T(8,128)(2,1)S(1)}, u32[]{:S(2)}, u32[]{:S(2)}) collective-permute-start(bf16[16,2048]{1,0:T(8,128)(2,1)S(1)} %shard_map.44.refs_2_), channel_id=1, source_target_pairs={{0,8},{8,0},{16,24},{24,16},{1,9},{9,1},{17,25},{25,17},{2,10},{10... | collective-permute-start | bytes 196616 | tf_op jit(solution)/shard_map/ppermute | solution.py:199
  64.3 4.8 %collective-permute-start.5 = (bf16[16,2048]{1,0:T(8,128)(2,1)S(1)}, bf16[16,2048]{1,0:T(8,128)(2,1)S(1)}, u32[]{:S(2)}, u32[]{:S(2)}) collective-permute-start(bf16[16,2048]{1,0:T(8,128)(2,1)S(1)} %shard_map.40.refs_0_), channel_id=1, source_target_pairs={{0,8},{8,0},{16,24},{24,16},{1,9},{9,1},{17,25},{25,17},{2,10},{10... | collective-permute-start | bytes 196616 | tf_op jit(solution)/shard_map/ppermute | solution.py:199
